TPU v7x, 128 devices: a whole 4x4x4 slice. The times are simulated.
128 devices in a mesh: dp: 32 (over z, y, core), mp: 4 (over x).
Axes of the slice: x: 4, y: 4, z: 4, core: 2. Of those that a mesh axis runs over, the one named last changes fastest.
Arguments:
- features: bfloat16 [98304, 1024], P('dp'), may hold values from -6 to 6
- curvature: bfloat16 [98304, 4096], P('dp', 'mp'), may hold values from 0.099609375 to 2
- task_grad: float32 [1024, 4096], P('dp', 'mp'), may hold values from -6 to 6
Outputs:
- solution: float32 [1024, 4096], P('dp', 'mp')
- residual: float32 [1024, 4096], P('dp', 'mp')
All inputs are finite; a program needn't handle non-finite values.
Results may differ from a plain program's by a relative error of at most 0.0095.
The roundings to bfloat16 on the way count: a program that leaves them out, or rounds other values in their place, can miss the bound.
Values may be sent and summed in bfloat16 or wider, within the bound.
A program may use at most 64 MiB of HBM per device.

v0:
```python
import jax
import jax.numpy as jnp
from jax import lax
from jax.sharding import PartitionSpec as P

ITERS = 2


damp_coef = 0.5


def weigh_rows(curvature, projected):
    return (curvature * projected).astype(jnp.bfloat16)


def shards(features, curvature, task_grad):
    token_count = features.shape[0] * lax.axis_size("dp")

    def global_sums(values):
        return lax.psum(values, ("dp", "mp"))

    solution = jnp.zeros_like(task_grad)
    residual = task_grad
    direction = task_grad
    norm_now = jnp.sum(residual * residual)
    for turn in range(ITERS):
        dir_bf = direction.astype(jnp.bfloat16)
        gathered = lax.all_gather(dir_bf, "dp", axis=0, tiled=True)
        projected = jnp.dot(features, gathered, preferred_element_type=jnp.float32)
        weighted = weigh_rows(curvature, projected)
        summed = lax.psum_scatter(
            lax.dot_general(
                features, weighted, (((0,), (0,)), ((), ())), preferred_element_type=jnp.float32
            ),
            "dp",
            scatter_dimension=0,
            tiled=True,
        )
        curved = summed / token_count + damp_coef * direction
        pdot_local = jnp.sum(direction * curved)
        if turn == 0:
            norm_now, curv_dot = global_sums((norm_now, pdot_local))
        else:
            curv_dot = global_sums(pdot_local)
        step_len = norm_now / curv_dot
        solution = solution + step_len * direction
        residual = residual - step_len * curved
        if turn + 1 < ITERS:
            norm_next = global_sums(jnp.sum(residual * residual))
        if turn + 1 < ITERS:
            direction = residual + norm_next / norm_now * direction
            norm_now = norm_next
    return (solution, residual)


def solution(mesh):
    placed = (P("dp", None), P("dp", "mp"), P("dp", "mp"))
    return jax.shard_map(
        shards,
        mesh=mesh,
        in_specs=placed,
        out_specs=(P("dp", "mp"), P("dp", "mp")),
        check_vma=False,
    )
```

profile of v0, /device:TPU:1, one launch (start us, length us, event | category | flops | bytes accessed | tf_op | source)
XLA Modules:
  0.0 527.6 jit_solution(15309340547715633252)
XLA Ops:
  7.2 0.0 all-gather.3.cloned.1.call-start
  7.2 1.5 convert_element_type.17
  8.8 0.0 all-gather.3.cloned.1.call-update
  8.8 0.0 reduce-scatter.7.cloned.1.call-start
  8.8 49.4 %all-gather.3.cloned.1.call-done = bf16[1024,1024]{1,0:T(8,128)(2,1)} async-done(((bf16[32,1024]{1,0:T(8,128)(2,1)}), bf16[1024,1024]{1,0:T(8,128)(2,1)}) %all-gather.3.cloned.1.call-update) | async-done | bytes 2097168 | tf_op jit(solution)/shard_map/all_gather | solution.py:28
  58.2 22.5 %fusion.4 = f32[1024,1024]{0,1:T(8,128)} fusion(bf16[3072,1024]{1,0:T(8,128)(2,1)} %param.3, bf16[3072,1024]{1,0:T(8,128)(2,1)} %param.4, bf16[1024,1024]{1,0:T(8,128)(2,1)} %all-gather.3.cloned.1.call-done), kind=kOutput, calls=%fused_computation.6 | convolution fusion | flops 12894339072 | bytes 18874368 | tf_op jit(solution)/shard_map/dot_general | solution.py:32
  80.7 0.0 copy-start
  80.7 5.4 %copy.24 = f32[1024,1024]{1,0:T(8,128)} copy(f32[1024,1024]{0,1:T(8,128)} %fusion.4) | data formatting | bytes 8388608
  86.0 0.0 reduce-scatter.7.cloned.1.call-update
  86.1 0.0 all-gather.5.cloned.1.call-start
  86.1 79.7 %reduce-scatter.7.cloned.1.call-done = f32[32,1024]{1,0:T(8,128)} async-done(((f32[1024,1024]{1,0:T(8,128)}), f32[32,1024]{1,0:T(8,128)}) %reduce-scatter.7.cloned.1.call-update) | async-done | bytes 131088 | tf_op jit(solution)/shard_map/reduce_scatter | solution.py:31
  165.8 0.0 copy-done
  165.8 1.5 multiply_reduce_fusion.2
  167.4 65.9 %all-reduce = (f32[]{:T(128)}, f32[]{:T(128)}) all-reduce(f32[]{:T(128)} %get-tuple-element.7, f32[]{:T(128)} %get-tuple-element.6), channel_id=1, replica_groups=mesh['dp'=32,'mp'=4] {'dp','mp'}, use_global_device_ids=true, to_apply=%region_1.0 | all-reduce | flops 2 | bytes 16 | tf_op jit(solution)/shard_map/psum | solution.py:20
  234.7 1.5 multiply_reduce_fusion.1
  236.2 62.5 %psum.30 = f32[]{:T(128)} all-reduce(f32[]{:T(128)} %multiply_reduce_fusion.1), channel_id=1, replica_groups=mesh['dp'=32,'mp'=4] {'dp','mp'}, use_global_device_ids=true, to_apply=%region_6.0 | all-reduce | flops 1 | bytes 8 | tf_op jit(solution)/shard_map/psum | solution.py:20
  300.1 1.6 fusion.6
  301.7 0.0 all-gather.5.cloned.1.call-update
  301.7 0.0 reduce-scatter.9.cloned.1.call-start
  301.8 41.3 %all-gather.5.cloned.1.call-done = bf16[1024,1024]{1,0:T(8,128)(2,1)} async-done(((bf16[32,1024]{1,0:T(8,128)(2,1)}), bf16[1024,1024]{1,0:T(8,128)(2,1)}) %all-gather.5.cloned.1.call-update) | async-done | bytes 2097168 | tf_op jit(solution)/shard_map/all_gather | solution.py:28
  343.1 22.3 %fusion.5 = f32[1024,1024]{0,1:T(8,128)} fusion(bf16[3072,1024]{1,0:T(8,128)(2,1)} %param.3, bf16[3072,1024]{1,0:T(8,128)(2,1)} %param.4, bf16[1024,1024]{1,0:T(8,128)(2,1)} %all-gather.5.cloned.1.call-done), kind=kOutput, calls=%fused_computation.7 | convolution fusion | flops 12894339072 | bytes 18874368 | tf_op jit(solution)/shard_map/dot_general | solution.py:32
  365.3 0.0 copy-start.1
  365.4 5.4 %copy.26 = f32[1024,1024]{1,0:T(8,128)} copy(f32[1024,1024]{0,1:T(8,128)} %fusion.5) | data formatting | bytes 8388608
  370.7 0.0 reduce-scatter.9.cloned.1.call-update
  370.8 79.8 %reduce-scatter.9.cloned.1.call-done = f32[32,1024]{1,0:T(8,128)} async-done(((f32[1024,1024]{1,0:T(8,128)}), f32[32,1024]{1,0:T(8,128)}) %reduce-scatter.9.cloned.1.call-update) | async-done | bytes 131088 | tf_op jit(solution)/shard_map/reduce_scatter | solution.py:31
  450.5 0.0 copy-done.1
  450.5 1.6 multiply_reduce_fusion
  452.1 65.9 %psum.31 = f32[]{:T(128)} all-reduce(f32[]{:T(128)} %multiply_reduce_fusion), channel_id=1, replica_groups=mesh['dp'=32,'mp'=4] {'dp','mp'}, use_global_device_ids=true, to_apply=%region_9.0 | all-reduce | flops 1 | bytes 8 | tf_op jit(solution)/shard_map/psum | solution.py:20
  519.4 1.7 multiply_subtract_fusion
Async XLA Ops:
  7.2 51.0 %all-gather.3.cloned.1.call-start = ((), (), s32[]{:S(2)}) async-start(), calls=%async_computation.2 | async-start | bytes 2162688 | tf_op jit(solution)/shard_map/all_gather | solution.py:28
  8.8 157.1 %reduce-scatter.7.cloned.1.call-start = ((), (), s32[]{:S(2)}) async-start(), calls=%async_computation.4 | async-start | bytes 4325376 | tf_op jit(solution)/shard_map/reduce_scatter | solution.py:31
  80.7 85.2 %copy-start = (f32[32,1024]{1,0:T(8,128)S(1)}, f32[32,1024]{1,0:T(8,128)}, u32[]{:S(2)}) copy-start(f32[32,1024]{1,0:T(8,128)} %param.5) | copy-start | bytes 393220
  86.1 257.0 %all-gather.5.cloned.1.call-start = ((), (), s32[]{:S(2)}) async-start(), calls=%async_computation.3 | async-start | bytes 2162688 | tf_op jit(solution)/shard_map/all_gather | solution.py:28
  301.7 148.8 %reduce-scatter.9.cloned.1.call-start = ((), (), s32[]{:S(2)}) async-start(), calls=%async_computation.5 | async-start | bytes 4325376 | tf_op jit(solution)/shard_map/reduce_scatter | solution.py:31
  365.3 85.2 %copy-start.1 = (f32[32,1024]{1,0:T(8,128)S(1)}, f32[32,1024]{1,0:T(8,128)}, u32[]{:S(2)}) copy-start(f32[32,1024]{1,0:T(8,128)} %reduce-scatter.7.cloned.1.call-done) | copy-start | bytes 393220
Sparse Core Ops, SparseCore 0:
  10.8 47.3 all-gather.2
  86.2 79.5 reduce-scatter.6
  301.8 41.2 all-gather.4
  370.9 79.6 reduce-scatter.8
where the time goes:
time: 528 us
  waiting for transfers between devices  250 us (47%)
  blocking collectives  194 us (37%)
  matrix products  44.8 us (8%)
  between operations  17.8 us (3%)
  local copies, waits for them, and re-layouts  10.8 us (2%)
  other arithmetic  9.45 us (2%)
    psum x3, blocking collectives, global_sums(): return lax.psum(values, ('dp', 'mp'))  194 us
    reduce_scatter x2, waiting for transfers between devices, shards(): lax.psum_scatter(lax.dot_general(features, weighted, (((0,), (0,)), ((),...  160 us
    all_gather x2, waiting for transfers between devices, shards(): gathered = lax.all_gather(dir_bf, 'dp', axis=0, tiled=True)  90.7 us
    dot_general x2, matrix products, shards(): lax.dot_general(features, weighted, (((0,), (0,)), ((), ())), preferred_e...  44.8 us
    unnamed x6, local copies, waits for them, and re-layouts  10.8 us
  transfers between devices with their start and end apart: 4, of which 4 were waited for; matrix products, arithmetic and copies ran while one was open for 0% of the time, Pallas kernels for 0%

commit v1 on v0

v1 whole, which is shorter than its diff:
```python
import functools

import jax
import jax.numpy as jnp
from jax import lax
from jax.experimental import pallas as pl
from jax.experimental.pallas import tpu as pltpu
from jax.sharding import PartitionSpec as P

RING = 4
GROUP = 32
N_MP = 4
TOK = 3072
DIN = 1024
COLS = 1024
NB = 256
BLOCKS = COLS // NB
ROWS = DIN // GROUP
TOKENS = 98304.0
DAMP = 0.5
MC = 1536
MESH = pl.DeviceIdType.MESH
BF, F32 = jnp.bfloat16, jnp.float32


def kernel(
    f_h, c_h, g_h, sol_h, res_h,
    f, ft, cv, g, d, w, sol, vb, g_own, g_par, v, wt,
    acc, accb, d0, d0b, s, sb, rin, rinb, xy, xyb, t, r2in,
    row, tab, row2, tab2,
    ss, rs, ts, tr, ts2, tr2, ld,
):
    me = lax.axis_index("dp")
    mx = lax.axis_index("mp")
    c = lax.rem(me, 2)
    chip = me // 2
    z = chip // RING
    y = lax.rem(chip, RING)
    pa = (1 - c) * y + c * z
    pb = (1 - c) * z + c * y

    def a_at(k):
        q = lax.rem(pa + k, RING)
        return ((1 - c) * (z * RING + q) + c * (q * RING + y)) * 2 + c

    def b_at(k):
        q = lax.rem(pb + k, RING)
        return ((1 - c) * (q * RING + y) + c * (z * RING + q)) * 2 + c

    partner = me + 1 - 2 * c
    a_up, a_dn, a_op = a_at(1), a_at(3), a_at(2)
    b_up, b_dn, b_op = b_at(1), b_at(3), b_at(2)
    qa_up, qa_dn, qa_op = lax.rem(pa + 1, RING), lax.rem(pa + 3, RING), lax.rem(pa + 2, RING)
    qb_up, qb_dn, qb_op = lax.rem(pb + 1, RING), lax.rem(pb + 3, RING), lax.rem(pb + 2, RING)

    loads = [
        pltpu.make_async_copy(g_h.at[:, pl.ds(j * NB, NB)], g.at[j], ld.at[j])
        for j in range(BLOCKS)
    ]
    parts = 4
    f_loads = [
        pltpu.make_async_copy(
            f_h.at[pl.ds(k * (TOK // parts), TOK // parts)],
            f.at[pl.ds(k * (TOK // parts), TOK // parts)],
            ld.at[BLOCKS + k],
        )
        for k in range(parts)
    ]
    c_load = pltpu.make_async_copy(c_h, cv, ld.at[BLOCKS + parts])
    for x in (*loads, *f_loads, c_load):
        x.start()

    barrier = pltpu.get_barrier_semaphore()

    @pl.loop(1, GROUP)
    def _(k):
        pl.semaphore_signal(
            barrier, inc=1, device_id={"dp": lax.rem(me + k, GROUP)}, device_id_type=MESH
        )

    for k in range(1, N_MP):
        pl.semaphore_signal(
            barrier, inc=1, device_id={"mp": lax.rem(mx + k, N_MP)}, device_id_type=MESH
        )

    def copy(j, i, src, dst, dev):
        return pltpu.make_async_remote_copy(
            src_ref=src, dst_ref=dst, send_sem=ss.at[j, i], recv_sem=rs.at[j, i],
            device_id={"dp": dev}, device_id_type=MESH,
        )

    def send(j, i, src, dst, dev):
        copy(j, i, src, dst, dev).start()

    def got(j, i, dst):
        copy(j, i, dst, dst, partner).wait_recv()

    def sent(j, i, src):
        copy(j, i, src, src, partner).wait_send()

    def strip(buf, j, q):
        return buf.at[j, pl.ds(q * RING, RING)]

    def ag1(j):
        dst = g_own.at[j, pb * RING + pa]
        send(j, 0, vb.at[j], dst, a_up)
        send(j, 1, vb.at[j], dst, a_dn)
        send(j, 2, vb.at[j], dst, a_op)
        g_own[j, pb * RING + pa] = vb[j]

    def ag2(j):
        got(j, 0, g_own.at[j, pb * RING + qa_dn])
        got(j, 1, g_own.at[j, pb * RING + qa_up])
        got(j, 2, g_own.at[j, pb * RING + qa_op])
        mine = strip(g_own, j, pb)
        send(j, 3, mine, mine, b_up)
        send(j, 4, mine, mine, b_dn)
        send(j, 7, mine, strip(g_par, j, pb), partner)

    def ag3(j):
        below, above = strip(g_own, j, qb_dn), strip(g_own, j, qb_up)
        got(j, 3, below)
        half = g_own.at[j, pl.ds(qb_dn * RING, 2)]
        send(j, 5, half, half, b_up)
        send(j, 8, below, strip(g_par, j, qb_dn), partner)
        got(j, 4, above)
        half = g_own.at[j, pl.ds(qb_up * RING + 2, 2)]
        send(j, 6, half, half, b_dn)
        send(j, 9, above, strip(g_par, j, qb_up), partner)

    def ag4(j):
        got(j, 5, g_own.at[j, pl.ds(qb_op * RING, 2)])
        got(j, 6, g_own.at[j, pl.ds(qb_op * RING + 2, 2)])
        send(j, 10, strip(g_own, j, qb_op), strip(g_par, j, qb_op), partner)

    def ag5(j):
        got(j, 7, strip(g_par, j, pa))
        got(j, 8, strip(g_par, j, qa_dn))
        got(j, 9, strip(g_par, j, qa_up))
        got(j, 10, strip(g_par, j, qa_op))
        for zz in range(RING):
            for yy in range(RING):
                zy, yz = zz * RING + yy, yy * RING + zz
                v[j, zz, yy, c] = g_own[j, (1 - c) * zy + c * yz]
                v[j, zz, yy, 1 - c] = g_par[j, (1 - c) * yz + c * zy]

    def p1(j, m):
        r = pl.ds(m * MC, MC)
        cols = pl.ds(pl.multiple_of(j * NB, NB), NB)
        p = jnp.dot(f[r, :], v[j].reshape(DIN, NB), preferred_element_type=F32)
        wt[r, :] = (cv[r, cols].astype(F32) * p).astype(BF)

    def p2(j, h, low):
        out = jnp.dot(ft[pl.ds(h * (DIN // 2), DIN // 2), :], wt[...], preferred_element_type=F32)
        out = out.reshape(2, RING, 2, ROWS, NB)
        acc[j, pl.ds(2 * h, 2)] = out
        if low:
            accb[j, pl.ds(2 * h, 2)] = out.astype(BF)
            send(j, 11 + h, accb.at[j, pl.ds(2 * h, 2), :, 1 - c], d0b.at[j, pl.ds(2 * h, 2)], partner)
        else:
            send(j, 11 + h, acc.at[j, pl.ds(2 * h, 2), :, 1 - c], d0.at[j, pl.ds(2 * h, 2)], partner)

    def r1(j, low):
        src, inn, sm = (d0b, rinb, sb) if low else (d0, rin, s)
        for h in range(2):
            got(j, 11 + h, src.at[j, pl.ds(2 * h, 2)])
            for zz in (2 * h, 2 * h + 1):
                for yy in range(RING):
                    zy, yz = zz * RING + yy, yy * RING + zz
                    both = acc[j, zz, yy, c] + src[j, zz, yy].astype(F32)
                    s[j, (1 - c) * yz + c * zy] = both
                    if low:
                        sb[j, (1 - c) * yz + c * zy] = both.astype(BF)
        send(j, 13, sm.at[j, pl.ds(qa_op * RING, 2)], inn.at[j, 0], a_up)
        send(j, 14, sm.at[j, pl.ds(qa_op * RING + 2, 2)], inn.at[j, 1], a_dn)
        send(j, 15, sm.at[j, pl.ds(qa_up * RING + 2, 2)], inn.at[j, 2], a_up)
        send(j, 16, sm.at[j, pl.ds(qa_dn * RING, 2)], inn.at[j, 3], a_dn)

    def r2(j, low):
        inn, out = (rinb, xyb) if low else (rin, xy)
        got(j, 13, inn.at[j, 0])
        out[j, 0] = (inn[j, 0].astype(F32) + s[j, pl.ds(qa_up * RING, 2)]).astype(out.dtype)
        send(j, 17, out.at[j, 0], inn.at[j, 4], a_up)
        got(j, 14, inn.at[j, 1])
        out[j, 1] = (inn[j, 1].astype(F32) + s[j, pl.ds(qa_dn * RING + 2, 2)]).astype(out.dtype)
        send(j, 18, out.at[j, 1], inn.at[j, 5], a_dn)

    def r3(j, low):
        inn = rinb if low else rin
        for i in (15, 16, 17, 18):
            got(j, i, inn.at[j, i - 13])
        mine = s[j, pl.ds(pa * RING, RING)]
        t[j, pl.ds(0, 2)] = mine[:2] + (inn[j, 4].astype(F32) + inn[j, 3].astype(F32))
        t[j, pl.ds(2, 2)] = mine[2:] + (inn[j, 2].astype(F32) + inn[j, 5].astype(F32))
        send(j, 19, t.at[j, qb_up], r2in.at[j, 0], b_up)
        send(j, 20, t.at[j, qb_dn], r2in.at[j, 1], b_dn)
        send(j, 21, t.at[j, qb_op], r2in.at[j, 2], b_op)

    def r4(j):
        for i in (19, 20, 21):
            got(j, i, r2in.at[j, i - 19])
        total = (t[j, pb] + r2in[j, 2]) + (r2in[j, 0] + r2in[j, 1])
        w[j] = total / TOKENS + DAMP * d[j]

    def drain_gather():
        @pl.loop(0, BLOCKS)
        def _(j):
            for i in range(3):
                sent(j, i, vb.at[j])
            for i in (3, 4, 7, 8, 9, 10):
                sent(j, i, strip(g_own, j, 0))
            for i in (5, 6):
                sent(j, i, g_own.at[j, pl.ds(0, 2)])

    def drain(low):
        @pl.loop(0, BLOCKS)
        def _(j):
            for i in (11, 12):
                sent(j, i, (d0b if low else d0).at[j, pl.ds(0, 2)])
            for i in range(13, 19):
                sent(j, i, (rinb if low else rin).at[j, 0])
            for i in range(19, 22):
                sent(j, i, t.at[j, 0])

    def operator(first):
        low = not first

        def transpose(k0, k1):
            if first:

                @pl.loop(k0, k1)
                def _(k):
                    r = pl.ds(pl.multiple_of(k * 256, 256), 256)
                    ft[:, r] = f[r, :].T

        for j in range(BLOCKS):
            vb[j] = d[j].astype(BF)
        if first:
            pl.semaphore_wait(barrier, GROUP - 1 + N_MP - 1)

        @pl.loop(0, BLOCKS)
        def _(j):
            ag1(j)

        if first:
            f_loads[0].wait()
            f_loads[1].wait()
        transpose(0, 4)
        ag2(0)
        ag2(1)
        if first:
            f_loads[2].wait()
        transpose(4, 8)
        ag3(0)
        if first:
            f_loads[3].wait()
        transpose(8, 12)
        ag4(0)
        if first:
            c_load.wait()
        ag5(0)

        @pl.loop(0, BLOCKS)
        def _(j):
            p1(j, 0)

            @pl.when(j < BLOCKS - 1)
            def _():
                ag3(j + 1)

            p1(j, 1)

            @pl.when(j < BLOCKS - 1)
            def _():
                ag4(j + 1)

            @pl.when(j >= 1)
            def _():
                r1(j - 1, low)

            @pl.when(j >= 2)
            def _():
                r3(j - 2, low)

            p2(j, 0, low)

            @pl.when(j < BLOCKS - 2)
            def _():
                ag2(j + 2)

            p2(j, 1, low)

            @pl.when(j >= 1)
            def _():
                r2(j - 1, low)

            @pl.when(j >= 2)
            def _():
                r4(j - 2)

            @pl.when(j < BLOCKS - 1)
            def _():
                ag5(j + 1)

        last = BLOCKS - 1
        r1(last, low)
        r3(last - 1, low)
        r2(last, low)
        r4(last - 1)
        r3(last, low)
        r4(last)

    def total(x):
        return jnp.sum(jnp.sum(jnp.sum(x, axis=0), axis=0, keepdims=True), axis=1, keepdims=True)

    def put(buf, i, values):
        buf[i] = jnp.zeros((8, 128), F32)
        for k, x in enumerate(values):
            buf[i, pl.ds(k, 1), :] = jnp.broadcast_to(x, (1, 128))

    def exchange(turn, values, middle, meanwhile):
        put(row, turn, values)

        @pl.loop(1, GROUP)
        def _(k):
            pltpu.make_async_remote_copy(
                src_ref=row.at[turn], dst_ref=tab.at[turn, me],
                send_sem=ts.at[turn, k], recv_sem=tr.at[turn, me],
                device_id={"dp": lax.rem(me + k, GROUP)}, device_id_type=MESH,
            ).start()

        tab[turn, me] = row[turn]
        meanwhile()

        @pl.loop(1, GROUP)
        def _(k):
            q = lax.rem(me + k, GROUP)
            pltpu.make_async_remote_copy(
                src_ref=row.at[turn], dst_ref=tab.at[turn, q],
                send_sem=ts.at[turn, k], recv_sem=tr.at[turn, q],
                device_id={"dp": q}, device_id_type=MESH,
            ).wait()

        put(row2, turn, middle(tab[turn]))
        out = [
            pltpu.make_async_remote_copy(
                src_ref=row2.at[turn], dst_ref=tab2.at[turn, mx],
                send_sem=ts2.at[turn, k], recv_sem=tr2.at[turn, k],
                device_id={"mp": lax.rem(mx + k, N_MP)}, device_id_type=MESH,
            )
            for k in range(1, N_MP)
        ]
        for x in out:
            x.start()
        tab2[turn, mx] = row2[turn]
        for k in range(1, N_MP):
            q = lax.rem(mx + N_MP - k, N_MP)
            pltpu.make_async_remote_copy(
                src_ref=row2.at[turn], dst_ref=tab2.at[turn, q],
                send_sem=ts2.at[turn, k], recv_sem=tr2.at[turn, k],
                device_id={"mp": q}, device_id_type=MESH,
            ).wait()
        return tab2[turn]

    def column(tb, k):
        return tb[:, k : k + 1, :]

    def moved(tb, x):
        ww, uu, uw, at = (column(tb, k) for k in (2, 3, 4, 5))
        gap = at - x
        return jnp.sum(uu + gap * (2.0 * uw + gap * ww), axis=0), jnp.sum(uw + gap * ww, axis=0)

    def ratio(p, q):
        return jnp.where(q > 0, p / jnp.where(q > 0, q, 1.0), 0.0)

    def centre(tb):
        gg, gw, ww = (jnp.sum(column(tb, k), axis=0) for k in range(3))
        x = ratio(gw, ww)
        uu, uw = moved(tb, x)
        return gg, gw, ww, uu, uw, x

    for x in loads:
        x.wait()
    d[...] = g[...]
    operator(True)
    gv, wv = g[...], w[...]
    gg, gw, ww = total(gv * gv), total(gv * wv), total(wv * wv)
    x = ratio(gw, ww)
    u = gv - x * wv
    drain_gather()
    tb = exchange(0, (gg, gw, ww, total(u * u), total(u * wv), x), centre, lambda: drain(False))
    norm = jnp.sum(column(tb, 0), axis=0)
    step = norm / jnp.sum(column(tb, 1), axis=0)
    norm_next, _ = moved(tb, step)
    beta = norm_next / norm
    step = step[:, :1]
    sol[...] = step * gv
    res = gv - step * wv
    g[...] = res
    d[...] = res + beta[:, :1] * gv
    operator(False)
    dv, wv = d[...], w[...]
    tb = exchange(1, (total(dv * wv),), lambda tb: (jnp.sum(column(tb, 0), axis=0),), lambda: drain(True))
    step = (norm_next / jnp.sum(column(tb, 0), axis=0))[:, :1]
    sol[...] = sol[...] + step * dv
    g[...] = g[...] - step * wv
    outs = [
        pltpu.make_async_copy(b.at[j], o.at[:, pl.ds(j * NB, NB)], ld.at[k * BLOCKS + j])
        for k, (b, o) in enumerate(((sol, sol_h), (g, res_h)))
        for j in range(BLOCKS)
    ]
    for x in outs:
        x.start()
    drain_gather()
    for x in outs:
        x.wait()


def shards(features, curvature, task_grad):
    any_spec = pl.BlockSpec(memory_space=pl.ANY)
    out = jax.ShapeDtypeStruct(task_grad.shape, F32)
    small = (BLOCKS, ROWS, NB)
    return pl.pallas_call(
        kernel,
        out_shape=(out, out),
        in_specs=[any_spec] * 3,
        out_specs=(any_spec, any_spec),
        scratch_shapes=[
            pltpu.VMEM((TOK, DIN), BF),
            pltpu.VMEM((DIN, TOK), BF),
            pltpu.VMEM((TOK, COLS), BF),
            pltpu.VMEM(small, F32),
            pltpu.VMEM(small, F32),
            pltpu.VMEM(small, F32),
            pltpu.VMEM(small, F32),
            pltpu.VMEM(small, BF),
            pltpu.VMEM((BLOCKS, 16, ROWS, NB), BF),
            pltpu.VMEM((BLOCKS, 16, ROWS, NB), BF),
            pltpu.VMEM((BLOCKS, RING, RING, 2, ROWS, NB), BF),
            pltpu.VMEM((TOK, NB), BF),
            pltpu.VMEM((BLOCKS, RING, RING, 2, ROWS, NB), F32),
            pltpu.VMEM((BLOCKS, RING, RING, 2, ROWS, NB), BF),
            pltpu.VMEM((BLOCKS, RING, RING, ROWS, NB), F32),
            pltpu.VMEM((BLOCKS, RING, RING, ROWS, NB), BF),
            pltpu.VMEM((BLOCKS, 16, ROWS, NB), F32),
            pltpu.VMEM((BLOCKS, 16, ROWS, NB), BF),
            pltpu.VMEM((BLOCKS, 6, 2, ROWS, NB), F32),
            pltpu.VMEM((BLOCKS, 6, 2, ROWS, NB), BF),
            pltpu.VMEM((BLOCKS, 2, 2, ROWS, NB), F32),
            pltpu.VMEM((BLOCKS, 2, 2, ROWS, NB), BF),
            pltpu.VMEM((BLOCKS, RING, ROWS, NB), F32),
            pltpu.VMEM((BLOCKS, 3, ROWS, NB), F32),
            pltpu.VMEM((2, 8, 128), F32),
            pltpu.VMEM((2, GROUP, 8, 128), F32),
            pltpu.VMEM((2, 8, 128), F32),
            pltpu.VMEM((2, N_MP, 8, 128), F32),
            pltpu.SemaphoreType.DMA((BLOCKS, 22)),
            pltpu.SemaphoreType.DMA((BLOCKS, 22)),
            pltpu.SemaphoreType.DMA((2, GROUP)),
            pltpu.SemaphoreType.DMA((2, GROUP)),
            pltpu.SemaphoreType.DMA((2, N_MP)),
            pltpu.SemaphoreType.DMA((2, N_MP)),
            pltpu.SemaphoreType.DMA((2 * BLOCKS + 1,)),
        ],
        compiler_params=pltpu.CompilerParams(
            collective_id=0, has_side_effects=True, vmem_limit_bytes=62 * 2**20
        ),
    )(features, curvature, task_grad)


def solution(mesh):
    placed = (P("dp", None), P("dp", "mp"), P("dp", "mp"))
    return jax.shard_map(
        shards,
        mesh=mesh,
        in_specs=placed,
        out_specs=(P("dp", "mp"), P("dp", "mp")),
        check_vma=False,
    )
```

time: 528 us -> 150 us (0.28)
  waiting for transfers between devices: 250 us -> 0 us
  blocking collectives: 194 us -> 0 us
  Pallas kernels: 0 us -> 146 us
  matrix products: 44.8 us -> 0 us
  between operations: 17.8 us -> 0.64 us
  other arithmetic: 9.45 us -> 0 us
  local copies, waits for them, and re-layouts: 10.8 us -> 3.14 us
    psum x3 -> x0, blocking collectives: 194 us -> none  [global_sums(): return lax.psum(values, ('dp', 'mp'))]
    reduce_scatter x2 -> x0, waiting for transfers between devices: 160 us -> none  [shards(): lax.psum_scatter(lax.dot_general(features, weighted, (((0,), (0,)), ((),...]
    pallas_call x0 -> x1, Pallas kernels: none -> 146 us  [shards(): pl.pallas_call(kernel, out_shape=(out, out), in_specs=[any_spec] * 3, out...]
    all_gather x2 -> x0, waiting for transfers between devices: 90.7 us -> none  [shards(): gathered = lax.all_gather(dir_bf, 'dp', axis=0, tiled=True)]
    dot_general x2 -> x0, matrix products: 44.8 us -> none  [shards(): lax.dot_general(features, weighted, (((0,), (0,)), ((), ())), preferred_e...]
    unnamed x6 -> x2, local copies, waits for them, and re-layouts: 10.8 us -> 3.14 us
  transfers between devices with their start and end apart: 4 -> 0, of which waited for: 4 -> 0; matrix products, arithmetic and copies ran while one was open for 0% -> 0% of each run, Pallas kernels for 0% -> 0%
where the time goes in v1:
time: 150 us
  Pallas kernels  146 us (97%)
  local copies, waits for them, and re-layouts  3.14 us (2%)
    pallas_call x1, Pallas kernels, shards(): pl.pallas_call(kernel, out_shape=(out, out), in_specs=[any_spec] * 3, out...  146 us
    unnamed x2, local copies, waits for them, and re-layouts  3.14 us

profile of v1, /device:TPU:1, one launch (start us, length us, event | category | flops | bytes accessed | tf_op | source)
XLA Modules:
  0.0 149.7 jit_solution(2369271796018558096)
XLA Ops:
  0.6 145.9 %shard_map.50 = (f32[32,1024]{1,0:T(8,128)}, f32[32,1024]{1,0:T(8,128)}) custom-call(bf16[3072,1024]{1,0:T(8,128)(2,1)} %f_h.1, bf16[3072,1024]{1,0:T(8,128)(2,1)} %c_h.1, f32[32,1024]{1,0:T(8,128)} %g_h.1), custom_call_target="tpu_custom_call" | custom-call | tf_op jit(solution)/shard_map/pallas_call | solution.py:423
  146.5 1.6 %copy.7 = f32[32,1024]{1,0:T(8,128)} copy(f32[32,1024]{1,0:T(8,128)} %get-tuple-element.4) | data formatting | bytes 262144
  148.1 1.6 %copy.8 = f32[32,1024]{1,0:T(8,128)} copy(f32[32,1024]{1,0:T(8,128)} %get-tuple-element.5) | data formatting | bytes 262144

commit v2 on v1

--- a/solution.py
+++ b/solution.py
@@ -26,7 +26,7 @@
 def kernel(
     f_h, c_h, g_h, sol_h, res_h,
     f, ft, cv, g, d, w, sol, vb, g_own, g_par, v, wt,
-    acc, accb, d0, d0b, s, sb, rin, rinb, xy, xyb, t, r2in,
+    acc, accb, d0, d0b, s, sb, rin, rinb, t, r2in,
     row, tab, row2, tab2,
     ss, rs, ts, tr, ts2, tr2, ld,
 ):
@@ -72,11 +72,8 @@
 
     barrier = pltpu.get_barrier_semaphore()
 
-    @pl.loop(1, GROUP)
-    def _(k):
-        pl.semaphore_signal(
-            barrier, inc=1, device_id={"dp": lax.rem(me + k, GROUP)}, device_id_type=MESH
-        )
+    for q in (a_up, a_dn, a_op, b_up, b_dn, b_op, partner):
+        pl.semaphore_signal(barrier, inc=1, device_id={"dp": q}, device_id_type=MESH)
 
     for k in range(1, N_MP):
         pl.semaphore_signal(
@@ -115,55 +112,56 @@
         mine = strip(g_own, j, pb)
         send(j, 3, mine, mine, b_up)
         send(j, 4, mine, mine, b_dn)
-        send(j, 7, mine, strip(g_par, j, pb), partner)
+        send(j, 5, mine, mine, b_op)
+        send(j, 6, mine, strip(g_par, j, pb), partner)
 
     def ag3(j):
-        below, above = strip(g_own, j, qb_dn), strip(g_own, j, qb_up)
-        got(j, 3, below)
-        half = g_own.at[j, pl.ds(qb_dn * RING, 2)]
-        send(j, 5, half, half, b_up)
-        send(j, 8, below, strip(g_par, j, qb_dn), partner)
-        got(j, 4, above)
-        half = g_own.at[j, pl.ds(qb_up * RING + 2, 2)]
-        send(j, 6, half, half, b_dn)
-        send(j, 9, above, strip(g_par, j, qb_up), partner)
-
-    def ag4(j):
-        got(j, 5, g_own.at[j, pl.ds(qb_op * RING, 2)])
-        got(j, 6, g_own.at[j, pl.ds(qb_op * RING + 2, 2)])
-        send(j, 10, strip(g_own, j, qb_op), strip(g_par, j, qb_op), partner)
+        for i, q in ((3, qb_dn), (4, qb_up), (5, qb_op)):
+            got(j, i, strip(g_own, j, q))
+            send(j, i + 4, strip(g_own, j, q), strip(g_par, j, q), partner)
 
     def ag5(j):
-        got(j, 7, strip(g_par, j, pa))
-        got(j, 8, strip(g_par, j, qa_dn))
-        got(j, 9, strip(g_par, j, qa_up))
-        got(j, 10, strip(g_par, j, qa_op))
+        got(j, 6, strip(g_par, j, pa))
+        got(j, 7, strip(g_par, j, qa_dn))
+        got(j, 8, strip(g_par, j, qa_up))
+        got(j, 9, strip(g_par, j, qa_op))
         for zz in range(RING):
             for yy in range(RING):
                 zy, yz = zz * RING + yy, yy * RING + zz
                 v[j, zz, yy, c] = g_own[j, (1 - c) * zy + c * yz]
                 v[j, zz, yy, 1 - c] = g_par[j, (1 - c) * yz + c * zy]
 
+    def alone(j):
+        return pl.loop(0, (j + BLOCKS) // BLOCKS)
+
     def p1(j, m):
         r = pl.ds(m * MC, MC)
         cols = pl.ds(pl.multiple_of(j * NB, NB), NB)
-        p = jnp.dot(f[r, :], v[j].reshape(DIN, NB), preferred_element_type=F32)
-        wt[r, :] = (cv[r, cols].astype(F32) * p).astype(BF)
+
+        @alone(j)
+        def _(_):
+            p = jnp.dot(f[r, :], v[j].reshape(DIN, NB), preferred_element_type=F32)
+            wt[r, :] = (cv[r, cols].astype(F32) * p).astype(BF)
 
     def p2(j, h, low):
-        out = jnp.dot(ft[pl.ds(h * (DIN // 2), DIN // 2), :], wt[...], preferred_element_type=F32)
-        out = out.reshape(2, RING, 2, ROWS, NB)
-        acc[j, pl.ds(2 * h, 2)] = out
-        if low:
-            accb[j, pl.ds(2 * h, 2)] = out.astype(BF)
-            send(j, 11 + h, accb.at[j, pl.ds(2 * h, 2), :, 1 - c], d0b.at[j, pl.ds(2 * h, 2)], partner)
-        else:
-            send(j, 11 + h, acc.at[j, pl.ds(2 * h, 2), :, 1 - c], d0.at[j, pl.ds(2 * h, 2)], partner)
+        r = pl.ds(h * (DIN // 2), DIN // 2)
+        zs = pl.ds(2 * h, 2)
+
+        @alone(j)
+        def _(_):
+            out = jnp.dot(ft[r, :], wt[...], preferred_element_type=F32)
+            out = out.reshape(2, RING, 2, ROWS, NB)
+            acc[j, zs] = out
+            if low:
+                accb[j, zs] = out.astype(BF)
+
+        src, dst = (accb, d0b) if low else (acc, d0)
+        send(j, 10 + h, src.at[j, zs, :, 1 - c], dst.at[j, zs], partner)
 
     def r1(j, low):
         src, inn, sm = (d0b, rinb, sb) if low else (d0, rin, s)
         for h in range(2):
-            got(j, 11 + h, src.at[j, pl.ds(2 * h, 2)])
+            got(j, 10 + h, src.at[j, pl.ds(2 * h, 2)])
             for zz in (2 * h, 2 * h + 1):
                 for yy in range(RING):
                     zy, yz = zz * RING + yy, yy * RING + zz
@@ -171,34 +169,23 @@
                     s[j, (1 - c) * yz + c * zy] = both
                     if low:
                         sb[j, (1 - c) * yz + c * zy] = both.astype(BF)
-        send(j, 13, sm.at[j, pl.ds(qa_op * RING, 2)], inn.at[j, 0], a_up)
-        send(j, 14, sm.at[j, pl.ds(qa_op * RING + 2, 2)], inn.at[j, 1], a_dn)
-        send(j, 15, sm.at[j, pl.ds(qa_up * RING + 2, 2)], inn.at[j, 2], a_up)
-        send(j, 16, sm.at[j, pl.ds(qa_dn * RING, 2)], inn.at[j, 3], a_dn)
-
-    def r2(j, low):
-        inn, out = (rinb, xyb) if low else (rin, xy)
-        got(j, 13, inn.at[j, 0])
-        out[j, 0] = (inn[j, 0].astype(F32) + s[j, pl.ds(qa_up * RING, 2)]).astype(out.dtype)
-        send(j, 17, out.at[j, 0], inn.at[j, 4], a_up)
-        got(j, 14, inn.at[j, 1])
-        out[j, 1] = (inn[j, 1].astype(F32) + s[j, pl.ds(qa_dn * RING + 2, 2)]).astype(out.dtype)
-        send(j, 18, out.at[j, 1], inn.at[j, 5], a_dn)
+        send(j, 12, strip(sm, j, qa_up), inn.at[j, 0], a_up)
+        send(j, 13, strip(sm, j, qa_dn), inn.at[j, 1], a_dn)
+        send(j, 14, strip(sm, j, qa_op), inn.at[j, 2], a_op)
 
     def r3(j, low):
         inn = rinb if low else rin
-        for i in (15, 16, 17, 18):
-            got(j, i, inn.at[j, i - 13])
+        for i in range(3):
+            got(j, 12 + i, inn.at[j, i])
         mine = s[j, pl.ds(pa * RING, RING)]
-        t[j, pl.ds(0, 2)] = mine[:2] + (inn[j, 4].astype(F32) + inn[j, 3].astype(F32))
-        t[j, pl.ds(2, 2)] = mine[2:] + (inn[j, 2].astype(F32) + inn[j, 5].astype(F32))
-        send(j, 19, t.at[j, qb_up], r2in.at[j, 0], b_up)
-        send(j, 20, t.at[j, qb_dn], r2in.at[j, 1], b_dn)
-        send(j, 21, t.at[j, qb_op], r2in.at[j, 2], b_op)
+        t[j] = (mine + inn[j, 2].astype(F32)) + (inn[j, 0].astype(F32) + inn[j, 1].astype(F32))
+        send(j, 15, t.at[j, qb_up], r2in.at[j, 0], b_up)
+        send(j, 16, t.at[j, qb_dn], r2in.at[j, 1], b_dn)
+        send(j, 17, t.at[j, qb_op], r2in.at[j, 2], b_op)
 
     def r4(j):
-        for i in (19, 20, 21):
-            got(j, i, r2in.at[j, i - 19])
+        for i in range(3):
+            got(j, 15 + i, r2in.at[j, i])
         total = (t[j, pb] + r2in[j, 2]) + (r2in[j, 0] + r2in[j, 1])
         w[j] = total / TOKENS + DAMP * d[j]
 
@@ -207,19 +194,17 @@
         def _(j):
             for i in range(3):
                 sent(j, i, vb.at[j])
-            for i in (3, 4, 7, 8, 9, 10):
+            for i in range(3, 10):
                 sent(j, i, strip(g_own, j, 0))
-            for i in (5, 6):
-                sent(j, i, g_own.at[j, pl.ds(0, 2)])
 
     def drain(low):
         @pl.loop(0, BLOCKS)
         def _(j):
-            for i in (11, 12):
+            for i in (10, 11):
                 sent(j, i, (d0b if low else d0).at[j, pl.ds(0, 2)])
-            for i in range(13, 19):
+            for i in (12, 13, 14):
                 sent(j, i, (rinb if low else rin).at[j, 0])
-            for i in range(19, 22):
+            for i in (15, 16, 17):
                 sent(j, i, t.at[j, 0])
 
     def operator(first):
@@ -236,26 +221,23 @@
         for j in range(BLOCKS):
             vb[j] = d[j].astype(BF)
         if first:
-            pl.semaphore_wait(barrier, GROUP - 1 + N_MP - 1)
-
-        @pl.loop(0, BLOCKS)
-        def _(j):
-            ag1(j)
-
+            pl.semaphore_wait(barrier, 7 + N_MP - 1)
+
+        ag1(0)
+        ag1(1)
         if first:
             f_loads[0].wait()
             f_loads[1].wait()
-        transpose(0, 4)
+        transpose(0, 6)
         ag2(0)
+        ag1(2)
+        ag1(3)
         ag2(1)
         if first:
             f_loads[2].wait()
-        transpose(4, 8)
+            f_loads[3].wait()
+        transpose(6, 12)
         ag3(0)
-        if first:
-            f_loads[3].wait()
-        transpose(8, 12)
-        ag4(0)
         if first:
             c_load.wait()
         ag5(0)
@@ -268,44 +250,35 @@
             def _():
                 ag3(j + 1)
 
+            @pl.when(j >= 1)
+            def _():
+                r1(j - 1, low)
+
             p1(j, 1)
 
+            @pl.when(j < BLOCKS - 2)
+            def _():
+                ag2(j + 2)
+
+            @pl.when(j >= 2)
+            def _():
+                r3(j - 2, low)
+
+            p2(j, 0, low)
+
             @pl.when(j < BLOCKS - 1)
             def _():
-                ag4(j + 1)
-
-            @pl.when(j >= 1)
-            def _():
-                r1(j - 1, low)
+                ag5(j + 1)
+
+            p2(j, 1, low)
 
             @pl.when(j >= 2)
             def _():
-                r3(j - 2, low)
-
-            p2(j, 0, low)
-
-            @pl.when(j < BLOCKS - 2)
-            def _():
-                ag2(j + 2)
-
-            p2(j, 1, low)
-
-            @pl.when(j >= 1)
-            def _():
-                r2(j - 1, low)
-
-            @pl.when(j >= 2)
-            def _():
                 r4(j - 2)
-
-            @pl.when(j < BLOCKS - 1)
-            def _():
-                ag5(j + 1)
 
         last = BLOCKS - 1
         r1(last, low)
         r3(last - 1, low)
-        r2(last, low)
         r4(last - 1)
         r3(last, low)
         r4(last)
@@ -444,18 +417,16 @@
             pltpu.VMEM((BLOCKS, RING, RING, ROWS, NB), BF),
             pltpu.VMEM((BLOCKS, 16, ROWS, NB), F32),
             pltpu.VMEM((BLOCKS, 16, ROWS, NB), BF),
-            pltpu.VMEM((BLOCKS, 6, 2, ROWS, NB), F32),
-            pltpu.VMEM((BLOCKS, 6, 2, ROWS, NB), BF),
-            pltpu.VMEM((BLOCKS, 2, 2, ROWS, NB), F32),
-            pltpu.VMEM((BLOCKS, 2, 2, ROWS, NB), BF),
+            pltpu.VMEM((BLOCKS, 3, RING, ROWS, NB), F32),
+            pltpu.VMEM((BLOCKS, 3, RING, ROWS, NB), BF),
             pltpu.VMEM((BLOCKS, RING, ROWS, NB), F32),
             pltpu.VMEM((BLOCKS, 3, ROWS, NB), F32),
             pltpu.VMEM((2, 8, 128), F32),
             pltpu.VMEM((2, GROUP, 8, 128), F32),
             pltpu.VMEM((2, 8, 128), F32),
             pltpu.VMEM((2, N_MP, 8, 128), F32),
-            pltpu.SemaphoreType.DMA((BLOCKS, 22)),
-            pltpu.SemaphoreType.DMA((BLOCKS, 22)),
+            pltpu.SemaphoreType.DMA((BLOCKS, 18)),
+            pltpu.SemaphoreType.DMA((BLOCKS, 18)),
             pltpu.SemaphoreType.DMA((2, GROUP)),
             pltpu.SemaphoreType.DMA((2, GROUP)),
             pltpu.SemaphoreType.DMA((2, N_MP)),

time: 150 us -> 118 us (0.79)
  Pallas kernels: 146 us -> 114 us
    pallas_call x1, Pallas kernels: 146 us -> 114 us  [shards(): pl.pallas_call(kernel, out_shape=(out, out), in_specs=[any_spec] * 3, out...]
where the time goes in v2:
time: 118 us
  Pallas kernels  114 us (97%)
  local copies, waits for them, and re-layouts  3.14 us (3%)
    pallas_call x1, Pallas kernels, shards(): pl.pallas_call(kernel, out_shape=(out, out), in_specs=[any_spec] * 3, out...  114 us
    unnamed x2, local copies, waits for them, and re-layouts  3.14 us

profile of v2, /device:TPU:1, one launch (start us, length us, event | category | flops | bytes accessed | tf_op | source)
XLA Modules:
  0.0 118.1 jit_solution(17156435515048830720)
XLA Ops:
  0.6 114.3 %shard_map.50 = (f32[32,1024]{1,0:T(8,128)}, f32[32,1024]{1,0:T(8,128)}) custom-call(bf16[3072,1024]{1,0:T(8,128)(2,1)} %f_h.1, bf16[3072,1024]{1,0:T(8,128)(2,1)} %c_h.1, f32[32,1024]{1,0:T(8,128)} %g_h.1), custom_call_target="tpu_custom_call" | custom-call | tf_op jit(solution)/shard_map/pallas_call | solution.py:396
  115.0 1.6 %copy.7 = f32[32,1024]{1,0:T(8,128)} copy(f32[32,1024]{1,0:T(8,128)} %get-tuple-element.4) | data formatting | bytes 262144
  116.6 1.6 %copy.8 = f32[32,1024]{1,0:T(8,128)} copy(f32[32,1024]{1,0:T(8,128)} %get-tuple-element.5) | data formatting | bytes 262144

commit v3 on v2

--- a/solution.py
+++ b/solution.py
@@ -24,11 +24,11 @@
 
 
 def kernel(
-    f_h, c_h, g_h, sol_h, res_h,
+    f_h, c_h, g_h, sol_o, res_o,
     f, ft, cv, g, d, w, sol, vb, g_own, g_par, v, wt,
     acc, accb, d0, d0b, s, sb, rin, rinb, t, r2in,
-    row, tab, row2, tab2,
-    ss, rs, ts, tr, ts2, tr2, ld,
+    xsrc, xo, xp, pdv, row, tab, row2, tab2,
+    ss, rs, xs, xr, ts, tr, ts2, tr2, ld,
 ):
     me = lax.axis_index("dp")
     mx = lax.axis_index("mp")
@@ -98,38 +98,76 @@
     def strip(buf, j, q):
         return buf.at[j, pl.ds(q * RING, RING)]
 
-    def ag1(j):
-        dst = g_own.at[j, pb * RING + pa]
-        send(j, 0, vb.at[j], dst, a_up)
-        send(j, 1, vb.at[j], dst, a_dn)
-        send(j, 2, vb.at[j], dst, a_op)
-        g_own[j, pb * RING + pa] = vb[j]
-
-    def ag2(j):
-        got(j, 0, g_own.at[j, pb * RING + qa_dn])
-        got(j, 1, g_own.at[j, pb * RING + qa_up])
-        got(j, 2, g_own.at[j, pb * RING + qa_op])
-        mine = strip(g_own, j, pb)
-        send(j, 3, mine, mine, b_up)
-        send(j, 4, mine, mine, b_dn)
-        send(j, 5, mine, mine, b_op)
-        send(j, 6, mine, strip(g_par, j, pb), partner)
-
-    def ag3(j):
-        for i, q in ((3, qb_dn), (4, qb_up), (5, qb_op)):
-            got(j, i, strip(g_own, j, q))
-            send(j, i + 4, strip(g_own, j, q), strip(g_par, j, q), partner)
-
-    def ag5(j):
-        got(j, 6, strip(g_par, j, pa))
-        got(j, 7, strip(g_par, j, qa_dn))
-        got(j, 8, strip(g_par, j, qa_up))
-        got(j, 9, strip(g_par, j, qa_op))
+    class Gather:
+        def __init__(self, src, own, par, sends, recvs):
+            self.src, self.own, self.par, self.sends, self.recvs = src, own, par, sends, recvs
+
+        def copy(self, j, i, src, dst, dev):
+            return pltpu.make_async_remote_copy(
+                src_ref=src, dst_ref=dst, send_sem=self.sends.at[j, i], recv_sem=self.recvs.at[j, i],
+                device_id={"dp": dev}, device_id_type=MESH,
+            )
+
+        def got(self, j, i, dst):
+            self.copy(j, i, dst, dst, partner).wait_recv()
+
+        def first(self, j):
+            at = pb * RING + pa
+            for i, dev in enumerate((a_up, a_dn, a_op)):
+                self.copy(j, i, self.src.at[j], self.own.at[j, at], dev).start()
+            self.own[j, at] = self.src[j]
+
+        def second(self, j):
+            for i, q in enumerate((qa_dn, qa_up, qa_op)):
+                self.got(j, i, self.own.at[j, pb * RING + q])
+            mine = strip(self.own, j, pb)
+            for i, dev in enumerate((b_up, b_dn, b_op)):
+                self.copy(j, 3 + i, mine, mine, dev).start()
+            self.copy(j, 6, mine, strip(self.par, j, pb), partner).start()
+
+        def third(self, j):
+            for i, q in enumerate((qb_dn, qb_up, qb_op)):
+                part = strip(self.own, j, q)
+                self.got(j, 3 + i, part)
+                self.copy(j, 7 + i, part, strip(self.par, j, q), partner).start()
+
+        def landed(self, j):
+            for i, q in enumerate((pa, qa_dn, qa_up, qa_op)):
+                self.got(j, 6 + i, strip(self.par, j, q))
+
+        def drain(self, j):
+            for i in range(10):
+                src = self.src.at[j] if i < 3 else strip(self.own, j, 0)
+                self.copy(j, i, src, src, partner).wait_send()
+
+    ag = Gather(vb, g_own, g_par, ss, rs)
+    xg = Gather(xsrc, xo, xp, xs, xr)
+
+    def places():
         for zz in range(RING):
             for yy in range(RING):
                 zy, yz = zz * RING + yy, yy * RING + zz
-                v[j, zz, yy, c] = g_own[j, (1 - c) * zy + c * yz]
-                v[j, zz, yy, 1 - c] = g_par[j, (1 - c) * yz + c * zy]
+                yield zz, yy, (1 - c) * zy + c * yz, (1 - c) * yz + c * zy
+
+    def fill(j):
+        ag.landed(j)
+        for zz, yy, mine, other in places():
+            v[j, zz, yy, c] = g_own[j, mine]
+            v[j, zz, yy, 1 - c] = g_par[j, other]
+
+    def local(j, step, beta):
+        for zz, yy, mine, other in places():
+            for buf, at, core in ((xo, mine, c), (xp, other, 1 - c)):
+                gv = buf[j, at]
+                nxt = (gv - step * buf[2 + j, at]) + beta * gv
+                buf[j, at] = nxt
+                v[j, zz, yy, core] = nxt.astype(BF)
+
+    def pd(j, slot):
+        part = jnp.zeros((ROWS, NB), F32)
+        for zz, yy, mine, other in places():
+            part += acc[j, zz, yy, c] * xo[slot, mine] + acc[j, zz, yy, 1 - c] * xp[slot, other]
+        pdv[j] = part
 
     def alone(j):
         return pl.loop(0, (j + BLOCKS) // BLOCKS)
@@ -189,14 +227,6 @@
         total = (t[j, pb] + r2in[j, 2]) + (r2in[j, 0] + r2in[j, 1])
         w[j] = total / TOKENS + DAMP * d[j]
 
-    def drain_gather():
-        @pl.loop(0, BLOCKS)
-        def _(j):
-            for i in range(3):
-                sent(j, i, vb.at[j])
-            for i in range(3, 10):
-                sent(j, i, strip(g_own, j, 0))
-
     def drain(low):
         @pl.loop(0, BLOCKS)
         def _(j):
@@ -207,40 +237,39 @@
             for i in (15, 16, 17):
                 sent(j, i, t.at[j, 0])
 
-    def operator(first):
-        low = not first
-
-        def transpose(k0, k1):
-            if first:
-
-                @pl.loop(k0, k1)
-                def _(k):
-                    r = pl.ds(pl.multiple_of(k * 256, 256), 256)
-                    ft[:, r] = f[r, :].T
-
+    def transpose(k0, k1):
+        @pl.loop(k0, k1)
+        def _(k):
+            r = pl.ds(pl.multiple_of(k * 256, 256), 256)
+            ft[:, r] = f[r, :].T
+
+    def operator_first():
         for j in range(BLOCKS):
             vb[j] = d[j].astype(BF)
-        if first:
-            pl.semaphore_wait(barrier, 7 + N_MP - 1)
-
-        ag1(0)
-        ag1(1)
-        if first:
-            f_loads[0].wait()
-            f_loads[1].wait()
+        for i in range(2):
+            xsrc[i] = g[i]
+        pl.semaphore_wait(barrier, 7 + N_MP - 1)
+        ag.first(0)
+        ag.first(1)
+        f_loads[0].wait()
+        f_loads[1].wait()
         transpose(0, 6)
-        ag2(0)
-        ag1(2)
-        ag1(3)
-        ag2(1)
-        if first:
-            f_loads[2].wait()
-            f_loads[3].wait()
+        ag.second(0)
+        ag.first(2)
+        ag.first(3)
+        ag.second(1)
+        xg.first(0)
+        xg.first(1)
+        f_loads[2].wait()
+        f_loads[3].wait()
         transpose(6, 12)
-        ag3(0)
-        if first:
-            c_load.wait()
-        ag5(0)
+        ag.third(0)
+        ag.second(2)
+        ag.second(3)
+        xg.second(0)
+        xg.second(1)
+        c_load.wait()
+        fill(0)
 
         @pl.loop(0, BLOCKS)
         def _(j):
@@ -248,39 +277,129 @@
 
             @pl.when(j < BLOCKS - 1)
             def _():
-                ag3(j + 1)
+                ag.third(j + 1)
 
             @pl.when(j >= 1)
             def _():
-                r1(j - 1, low)
+                r1(j - 1, False)
 
             p1(j, 1)
 
-            @pl.when(j < BLOCKS - 2)
-            def _():
-                ag2(j + 2)
-
             @pl.when(j >= 2)
             def _():
-                r3(j - 2, low)
-
-            p2(j, 0, low)
+                r3(j - 2, False)
+
+            p2(j, 0, False)
 
             @pl.when(j < BLOCKS - 1)
             def _():
-                ag5(j + 1)
-
-            p2(j, 1, low)
+                fill(j + 1)
+
+            @pl.when((j >= 1) & (j < 3))
+            def _():
+                xg.third(j - 1)
+
+            @pl.when(j >= 3)
+            def _():
+                r4(j - 3)
+                xsrc[2] = w[0]
+                xg.first(2)
+
+            p2(j, 1, False)
+
+        last = BLOCKS - 1
+        r1(last, False)
+        r3(last - 1, False)
+        r4(last - 2)
+        xsrc[3] = w[1]
+        xg.first(3)
+        r3(last, False)
+        xg.second(2)
+        r4(last - 1)
+        r4(last)
+
+    def operator_second(step, beta):
+        for j in (2, 3):
+            vb[j] = d[j].astype(BF)
+            xsrc[2 + j] = d[j]
+        ag.first(2)
+        ag.first(3)
+        xg.first(4)
+        xg.first(5)
+        local(0, step, beta)
+
+        @pl.loop(0, BLOCKS)
+        def _(j):
+            p1(j, 0)
+
+            @pl.when(j >= 1)
+            def _():
+                r1(j - 1, True)
+
+            p1(j, 1)
+
+            @pl.when(j == 1)
+            def _():
+                ag.third(2)
+                pd(0, 0)
+
+            @pl.when(j == 2)
+            def _():
+                pd(1, 1)
+
+            @pl.when(j == 3)
+            def _():
+                xg.third(5)
+                xg.landed(4)
+                pd(2, 4)
 
             @pl.when(j >= 2)
             def _():
-                r4(j - 2)
+                r3(j - 2, True)
+
+            p2(j, 0, True)
+
+            @pl.when(j == 0)
+            def _():
+                local(1, step, beta)
+                ag.second(2)
+                ag.second(3)
+
+            @pl.when(j == 1)
+            def _():
+                ag.third(3)
+
+            @pl.when(j == 2)
+            def _():
+                xg.third(4)
+                fill(3)
+
+            @pl.when(j >= 3)
+            def _():
+                r4(j - 3)
+
+            p2(j, 1, True)
+
+            @pl.when(j == 0)
+            def _():
+                xg.second(4)
+                xg.second(5)
+
+            @pl.when(j == 1)
+            def _():
+                fill(2)
 
         last = BLOCKS - 1
-        r1(last, low)
-        r3(last - 1, low)
+        xg.landed(5)
+        pd(3, 5)
+        dv = d[...]
+        exchange_send(1, (total(pdv[...]) / TOKENS + DAMP * total(dv * dv),))
+        r1(last, True)
+        r3(last - 1, True)
+        r4(last - 2)
+        r3(last, True)
+        exchange_middle(1, lambda tb: (jnp.sum(column(tb, 0), axis=0),))
         r4(last - 1)
-        r3(last, low)
         r4(last)
 
     def total(x):
@@ -291,48 +410,42 @@
         for k, x in enumerate(values):
             buf[i, pl.ds(k, 1), :] = jnp.broadcast_to(x, (1, 128))
 
-    def exchange(turn, values, middle, meanwhile):
+    def to_group(turn, k, q):
+        return pltpu.make_async_remote_copy(
+            src_ref=row.at[turn], dst_ref=tab.at[turn, q],
+            send_sem=ts.at[turn, k], recv_sem=tr.at[turn, q],
+            device_id={"dp": lax.rem(me + k, GROUP)}, device_id_type=MESH,
+        )
+
+    def to_mp(turn, k, q):
+        return pltpu.make_async_remote_copy(
+            src_ref=row2.at[turn], dst_ref=tab2.at[turn, q],
+            send_sem=ts2.at[turn, k], recv_sem=tr2.at[turn, k],
+            device_id={"mp": lax.rem(mx + k, N_MP)}, device_id_type=MESH,
+        )
+
+    def exchange_send(turn, values):
         put(row, turn, values)
 
         @pl.loop(1, GROUP)
         def _(k):
-            pltpu.make_async_remote_copy(
-                src_ref=row.at[turn], dst_ref=tab.at[turn, me],
-                send_sem=ts.at[turn, k], recv_sem=tr.at[turn, me],
-                device_id={"dp": lax.rem(me + k, GROUP)}, device_id_type=MESH,
-            ).start()
+            to_group(turn, k, me).start()
 
         tab[turn, me] = row[turn]
-        meanwhile()
-
+
+    def exchange_middle(turn, middle):
         @pl.loop(1, GROUP)
         def _(k):
-            q = lax.rem(me + k, GROUP)
-            pltpu.make_async_remote_copy(
-                src_ref=row.at[turn], dst_ref=tab.at[turn, q],
-                send_sem=ts.at[turn, k], recv_sem=tr.at[turn, q],
-                device_id={"dp": q}, device_id_type=MESH,
-            ).wait()
+            to_group(turn, k, lax.rem(me + k, GROUP)).wait()
 
         put(row2, turn, middle(tab[turn]))
-        out = [
-            pltpu.make_async_remote_copy(
-                src_ref=row2.at[turn], dst_ref=tab2.at[turn, mx],
-                send_sem=ts2.at[turn, k], recv_sem=tr2.at[turn, k],
-                device_id={"mp": lax.rem(mx + k, N_MP)}, device_id_type=MESH,
-            )
-            for k in range(1, N_MP)
-        ]
-        for x in out:
-            x.start()
+        for k in range(1, N_MP):
+            to_mp(turn, k, mx).start()
         tab2[turn, mx] = row2[turn]
+
+    def exchange_end(turn):
         for k in range(1, N_MP):
-            q = lax.rem(mx + N_MP - k, N_MP)
-            pltpu.make_async_remote_copy(
-                src_ref=row2.at[turn], dst_ref=tab2.at[turn, q],
-                send_sem=ts2.at[turn, k], recv_sem=tr2.at[turn, k],
-                device_id={"mp": q}, device_id_type=MESH,
-            ).wait()
+            to_mp(turn, k, lax.rem(mx + N_MP - k, N_MP)).wait()
         return tab2[turn]
 
     def column(tb, k):
@@ -355,49 +468,55 @@
     for x in loads:
         x.wait()
     d[...] = g[...]
-    operator(True)
+    operator_first()
     gv, wv = g[...], w[...]
     gg, gw, ww = total(gv * gv), total(gv * wv), total(wv * wv)
     x = ratio(gw, ww)
     u = gv - x * wv
-    drain_gather()
-    tb = exchange(0, (gg, gw, ww, total(u * u), total(u * wv), x), centre, lambda: drain(False))
+    for j in range(BLOCKS):
+        ag.drain(j)
+    exchange_send(0, (gg, gw, ww, total(u * u), total(u * wv), x))
+    xg.second(3)
+    xg.third(2)
+    drain(False)
+    exchange_middle(0, centre)
+    xg.third(3)
+    for i in range(4):
+        xg.drain(i)
+        xg.landed(i)
+    tb = exchange_end(0)
     norm = jnp.sum(column(tb, 0), axis=0)
     step = norm / jnp.sum(column(tb, 1), axis=0)
     norm_next, _ = moved(tb, step)
-    beta = norm_next / norm
+    beta = (norm_next / norm)[:, :1]
     step = step[:, :1]
     sol[...] = step * gv
     res = gv - step * wv
     g[...] = res
-    d[...] = res + beta[:, :1] * gv
-    operator(False)
+    d[...] = res + beta * gv
+    operator_second(step, beta)
+    tb = exchange_end(1)
+    step = (norm_next / jnp.sum(column(tb, 0), axis=0))[:, :1]
     dv, wv = d[...], w[...]
-    tb = exchange(1, (total(dv * wv),), lambda tb: (jnp.sum(column(tb, 0), axis=0),), lambda: drain(True))
-    step = (norm_next / jnp.sum(column(tb, 0), axis=0))[:, :1]
-    sol[...] = sol[...] + step * dv
-    g[...] = g[...] - step * wv
-    outs = [
-        pltpu.make_async_copy(b.at[j], o.at[:, pl.ds(j * NB, NB)], ld.at[k * BLOCKS + j])
-        for k, (b, o) in enumerate(((sol, sol_h), (g, res_h)))
-        for j in range(BLOCKS)
-    ]
-    for x in outs:
-        x.start()
-    drain_gather()
-    for x in outs:
-        x.wait()
+    for j in range(BLOCKS):
+        cols = pl.ds(j * NB, NB)
+        sol_o[:, cols] = sol[j] + step * dv[j]
+        res_o[:, cols] = g[j] - step * wv[j]
+    drain(True)
+    for j in (2, 3):
+        ag.drain(j)
+        xg.drain(2 + j)
 
 
 def shards(features, curvature, task_grad):
-    any_spec = pl.BlockSpec(memory_space=pl.ANY)
+    any_spec = pl.BlockSpec(memory_space=pltpu.HBM)
     out = jax.ShapeDtypeStruct(task_grad.shape, F32)
     small = (BLOCKS, ROWS, NB)
     return pl.pallas_call(
         kernel,
         out_shape=(out, out),
         in_specs=[any_spec] * 3,
-        out_specs=(any_spec, any_spec),
+        out_specs=(pl.BlockSpec(memory_space=pltpu.VMEM),) * 2,
         scratch_shapes=[
             pltpu.VMEM((TOK, DIN), BF),
             pltpu.VMEM((DIN, TOK), BF),
@@ -421,12 +540,18 @@
             pltpu.VMEM((BLOCKS, 3, RING, ROWS, NB), BF),
             pltpu.VMEM((BLOCKS, RING, ROWS, NB), F32),
             pltpu.VMEM((BLOCKS, 3, ROWS, NB), F32),
+            pltpu.VMEM((6, ROWS, NB), F32),
+            pltpu.VMEM((6, 16, ROWS, NB), F32),
+            pltpu.VMEM((6, 16, ROWS, NB), F32),
+            pltpu.VMEM(small, F32),
             pltpu.VMEM((2, 8, 128), F32),
             pltpu.VMEM((2, GROUP, 8, 128), F32),
             pltpu.VMEM((2, 8, 128), F32),
             pltpu.VMEM((2, N_MP, 8, 128), F32),
             pltpu.SemaphoreType.DMA((BLOCKS, 18)),
             pltpu.SemaphoreType.DMA((BLOCKS, 18)),
+            pltpu.SemaphoreType.DMA((6, 10)),
+            pltpu.SemaphoreType.DMA((6, 10)),
             pltpu.SemaphoreType.DMA((2, GROUP)),
             pltpu.SemaphoreType.DMA((2, GROUP)),
             pltpu.SemaphoreType.DMA((2, N_MP)),
@@ -434,9 +559,9 @@
             pltpu.SemaphoreType.DMA((2 * BLOCKS + 1,)),
         ],
         compiler_params=pltpu.CompilerParams(
-            collective_id=0, has_side_effects=True, vmem_limit_bytes=62 * 2**20
+            collective_id=0, has_side_effects=True, vmem_limit_bytes=51 * 2**20
         ),
-    )(features, curvature, task_grad)
+    )(features, curvature, pltpu.with_memory_space_constraint(task_grad, pltpu.HBM))
 
 
 def solution(mesh):

time: 118 us -> 95.6 us (0.81)
  Pallas kernels: 114 us -> 93.6 us
  local copies, waits for them, and re-layouts: 3.14 us -> 1.31 us
    pallas_call x1, Pallas kernels: 114 us -> 93.6 us  [shards(): pl.pallas_call(kernel, out_shape=(out, out), in_specs=[any_spec] * 3, out...]
    unnamed x2, local copies, waits for them, and re-layouts: 3.14 us -> 1.31 us
where the time goes in v3:
time: 95.6 us; the launch traced here: 95.5 us
  Pallas kernels  93.6 us (98%)
  local copies, waits for them, and re-layouts  1.31 us (1%)
    pallas_call x1, Pallas kernels, shards(): pl.pallas_call(kernel, out_shape=(out, out), in_specs=[any_spec] * 3, out...  93.6 us

profile of v3, /device:TPU:1, one launch (start us, length us, event | category | flops | bytes accessed | tf_op | source)
XLA Modules:
  0.0 95.5 jit_solution(10056670960633926533)
XLA Ops:
  0.6 93.6 %shard_map.50 = (f32[32,1024]{1,0:T(8,128)S(1)}, f32[32,1024]{1,0:T(8,128)S(1)}) custom-call(bf16[3072,1024]{1,0:T(8,128)(2,1)} %f_h.1, bf16[3072,1024]{1,0:T(8,128)(2,1)} %c_h.1, f32[32,1024]{1,0:T(8,128)} %g_h.1), custom_call_target="tpu_custom_call" | custom-call | tf_op jit(solution)/shard_map/pallas_call | solution.py:515
  94.2 0.7 copy.7
  94.8 0.7 copy.8

commit v4 on v3

--- a/solution.py
+++ b/solution.py
@@ -18,17 +18,20 @@
 ROWS = DIN // GROUP
 TOKENS = 98304.0
 DAMP = 0.5
-MC = 1536
 MESH = pl.DeviceIdType.MESH
 BF, F32 = jnp.bfloat16, jnp.float32
+FAR_FIRST = sorted(
+    ((i, k) for i in range(RING) for k in range(RING) if i or k),
+    key=lambda t: -min(t[0], RING - t[0]) - min(t[1], RING - t[1]),
+)
 
 
 def kernel(
     f_h, c_h, g_h, sol_o, res_o,
     f, ft, cv, g, d, w, sol, vb, g_own, g_par, v, wt,
-    acc, accb, d0, d0b, s, sb, rin, rinb, t, r2in,
-    xsrc, xo, xp, pdv, row, tab, row2, tab2,
-    ss, rs, xs, xr, ts, tr, ts2, tr2, ld,
+    acc, accb, d0, d0b, s, sb, rin, t, r2in,
+    din, xsrc, xo, xp, lsrc, lo, lp, pdv, row, tab, one_row, one_tab, row2, tab2,
+    ss, rs, xs, xr, ls, lr, ds, dr, ts, tr, ts2, tr2, ld,
 ):
     me = lax.axis_index("dp")
     mx = lax.axis_index("mp")
@@ -142,6 +145,7 @@
 
     ag = Gather(vb, g_own, g_par, ss, rs)
     xg = Gather(xsrc, xo, xp, xs, xr)
+    lg = Gather(lsrc, lo, lp, ls, lr)
 
     def places():
         for zz in range(RING):
@@ -163,23 +167,29 @@
                 buf[j, at] = nxt
                 v[j, zz, yy, core] = nxt.astype(BF)
 
-    def pd(j, slot):
+    def pd(j):
         part = jnp.zeros((ROWS, NB), F32)
         for zz, yy, mine, other in places():
-            part += acc[j, zz, yy, c] * xo[slot, mine] + acc[j, zz, yy, 1 - c] * xp[slot, other]
+            part += acc[j, zz, yy, c] * xo[j, mine] + acc[j, zz, yy, 1 - c] * xp[j, other]
+        pdv[j] = part
+
+    def pd_rest(j):
+        part = jnp.zeros((ROWS, NB), F32)
+        for zz, yy, mine, other in places():
+            for core, rest in ((c, lo[j - 2, mine]), (1 - c, lp[j - 2, other])):
+                part += acc[j, zz, yy, core] * (v[j, zz, yy, core].astype(F32) + rest.astype(F32))
         pdv[j] = part
 
     def alone(j):
         return pl.loop(0, (j + BLOCKS) // BLOCKS)
 
-    def p1(j, m):
-        r = pl.ds(m * MC, MC)
+    def p1(j):
         cols = pl.ds(pl.multiple_of(j * NB, NB), NB)
 
         @alone(j)
         def _(_):
-            p = jnp.dot(f[r, :], v[j].reshape(DIN, NB), preferred_element_type=F32)
-            wt[r, :] = (cv[r, cols].astype(F32) * p).astype(BF)
+            p = jnp.dot(f[...], v[j].reshape(DIN, NB), preferred_element_type=F32)
+            wt[...] = (cv[:, cols].astype(F32) * p).astype(BF)
 
     def p2(j, h, low):
         r = pl.ds(h * (DIN // 2), DIN // 2)
@@ -197,7 +207,7 @@
         send(j, 10 + h, src.at[j, zs, :, 1 - c], dst.at[j, zs], partner)
 
     def r1(j, low):
-        src, inn, sm = (d0b, rinb, sb) if low else (d0, rin, s)
+        src = d0b if low else d0
         for h in range(2):
             got(j, 10 + h, src.at[j, pl.ds(2 * h, 2)])
             for zz in (2 * h, 2 * h + 1):
@@ -207,16 +217,35 @@
                     s[j, (1 - c) * yz + c * zy] = both
                     if low:
                         sb[j, (1 - c) * yz + c * zy] = both.astype(BF)
-        send(j, 12, strip(sm, j, qa_up), inn.at[j, 0], a_up)
-        send(j, 13, strip(sm, j, qa_dn), inn.at[j, 1], a_dn)
-        send(j, 14, strip(sm, j, qa_op), inn.at[j, 2], a_op)
-
-    def r3(j, low):
-        inn = rinb if low else rin
+        if low:
+            for ka, kb in FAR_FIRST:
+                piece(j, ka, kb).start()
+        else:
+            send(j, 12, strip(s, j, qa_up), rin.at[j, 0], a_up)
+            send(j, 13, strip(s, j, qa_dn), rin.at[j, 1], a_dn)
+            send(j, 14, strip(s, j, qa_op), rin.at[j, 2], a_op)
+
+    def piece(j, ka, kb):
+        qa, qb = lax.rem(pa + ka, RING), lax.rem(pb + kb, RING)
+        dev = ((1 - c) * (qb * RING + qa) + c * (qa * RING + qb)) * 2 + c
+        return pltpu.make_async_remote_copy(
+            src_ref=sb.at[j, qa * RING + qb], dst_ref=din.at[j, ka * RING + kb],
+            send_sem=ds.at[j, ka * RING + kb], recv_sem=dr.at[j, ka * RING + kb],
+            device_id={"dp": dev}, device_id_type=MESH,
+        )
+
+    def r4_low(j):
+        total = s[j, pa * RING + pb]
+        for ka, kb in reversed(FAR_FIRST):
+            piece(j, ka, kb).wait_recv()
+            total += din[j, ka * RING + kb].astype(F32)
+        w[j] = total / TOKENS + DAMP * d[j]
+
+    def r3(j):
         for i in range(3):
-            got(j, 12 + i, inn.at[j, i])
+            got(j, 12 + i, rin.at[j, i])
         mine = s[j, pl.ds(pa * RING, RING)]
-        t[j] = (mine + inn[j, 2].astype(F32)) + (inn[j, 0].astype(F32) + inn[j, 1].astype(F32))
+        t[j] = (mine + rin[j, 2]) + (rin[j, 0] + rin[j, 1])
         send(j, 15, t.at[j, qb_up], r2in.at[j, 0], b_up)
         send(j, 16, t.at[j, qb_dn], r2in.at[j, 1], b_dn)
         send(j, 17, t.at[j, qb_op], r2in.at[j, 2], b_op)
@@ -232,10 +261,14 @@
         def _(j):
             for i in (10, 11):
                 sent(j, i, (d0b if low else d0).at[j, pl.ds(0, 2)])
-            for i in (12, 13, 14):
-                sent(j, i, (rinb if low else rin).at[j, 0])
-            for i in (15, 16, 17):
-                sent(j, i, t.at[j, 0])
+            if low:
+                for ka, kb in FAR_FIRST:
+                    piece(j, ka, kb).wait_send()
+            else:
+                for i in (12, 13, 14):
+                    sent(j, i, rin.at[j, 0])
+                for i in (15, 16, 17):
+                    sent(j, i, t.at[j, 0])
 
     def transpose(k0, k1):
         @pl.loop(k0, k1)
@@ -266,14 +299,12 @@
         ag.third(0)
         ag.second(2)
         ag.second(3)
-        xg.second(0)
-        xg.second(1)
         c_load.wait()
         fill(0)
 
         @pl.loop(0, BLOCKS)
         def _(j):
-            p1(j, 0)
+            p1(j)
 
             @pl.when(j < BLOCKS - 1)
             def _():
@@ -283,13 +314,16 @@
             def _():
                 r1(j - 1, False)
 
-            p1(j, 1)
+            @pl.when(j == 0)
+            def _():
+                xg.second(0)
+                xg.second(1)
+
+            p2(j, 0, False)
 
             @pl.when(j >= 2)
             def _():
-                r3(j - 2, False)
-
-            p2(j, 0, False)
+                r3(j - 2)
 
             @pl.when(j < BLOCKS - 1)
             def _():
@@ -309,61 +343,63 @@
 
         last = BLOCKS - 1
         r1(last, False)
-        r3(last - 1, False)
+        r3(last - 1)
         r4(last - 2)
         xsrc[3] = w[1]
         xg.first(3)
-        r3(last, False)
+        r3(last)
         xg.second(2)
         r4(last - 1)
         r4(last)
 
     def operator_second(step, beta):
         for j in (2, 3):
-            vb[j] = d[j].astype(BF)
-            xsrc[2 + j] = d[j]
+            near = d[j].astype(BF)
+            vb[j] = near
+            lsrc[j - 2] = (d[j] - near.astype(F32)).astype(BF)
         ag.first(2)
         ag.first(3)
-        xg.first(4)
-        xg.first(5)
+        lg.first(0)
+        lg.first(1)
         local(0, step, beta)
 
         @pl.loop(0, BLOCKS)
         def _(j):
-            p1(j, 0)
+            p1(j)
+
+            @pl.when(j == 0)
+            def _():
+                xg.third(3)
+
+            @pl.when(j == 1)
+            def _():
+                ag.third(2)
+                pd(0)
+
+            @pl.when(j == 2)
+            def _():
+                pd(1)
+
+            @pl.when(j == 3)
+            def _():
+                lg.third(1)
+                lg.landed(0)
+                pd_rest(2)
 
             @pl.when(j >= 1)
             def _():
                 r1(j - 1, True)
 
-            p1(j, 1)
-
-            @pl.when(j == 1)
-            def _():
-                ag.third(2)
-                pd(0, 0)
-
-            @pl.when(j == 2)
-            def _():
-                pd(1, 1)
-
-            @pl.when(j == 3)
-            def _():
-                xg.third(5)
-                xg.landed(4)
-                pd(2, 4)
-
-            @pl.when(j >= 2)
-            def _():
-                r3(j - 2, True)
-
             p2(j, 0, True)
 
             @pl.when(j == 0)
             def _():
-                local(1, step, beta)
+                xg.drain(1)
+                xg.landed(1)
+                xg.landed(3)
                 ag.second(2)
                 ag.second(3)
+                local(1, step, beta)
 
             @pl.when(j == 1)
             def _():
@@ -371,49 +407,65 @@
 
             @pl.when(j == 2)
             def _():
-                xg.third(4)
+                lg.third(0)
                 fill(3)
 
             @pl.when(j >= 3)
             def _():
-                r4(j - 3)
+                r4_low(j - 3)
 
             p2(j, 1, True)
 
             @pl.when(j == 0)
             def _():
-                xg.second(4)
-                xg.second(5)
+                lg.second(0)
+                lg.second(1)
 
             @pl.when(j == 1)
             def _():
                 fill(2)
 
         last = BLOCKS - 1
-        xg.landed(5)
-        pd(3, 5)
+        lg.landed(1)
+        pd_rest(3)
         dv = d[...]
-        exchange_send(1, (total(pdv[...]) / TOKENS + DAMP * total(dv * dv),))
+        value = total(pdv[...]) / TOKENS + DAMP * total(dv * dv)
+        one_row[...] = jnp.broadcast_to(value, (1, 128))
+
+        @pl.loop(1, GROUP)
+        def _(k):
+            one_to_group(k, me).start()
+
+        one_tab[me] = one_row[...]
         r1(last, True)
-        r3(last - 1, True)
-        r4(last - 2)
-        r3(last, True)
-        exchange_middle(1, lambda tb: (jnp.sum(column(tb, 0), axis=0),))
-        r4(last - 1)
-        r4(last)
+        r4_low(last - 2)
+
+        @pl.loop(1, GROUP)
+        def _(k):
+            one_to_group(k, lax.rem(me + k, GROUP)).wait()
+
+        put(row2.at[1], (jnp.sum(one_tab[...], axis=0),))
+        exchange_over_mp(1)
+        r4_low(last - 1)
+        r4_low(last)
 
     def total(x):
         return jnp.sum(jnp.sum(jnp.sum(x, axis=0), axis=0, keepdims=True), axis=1, keepdims=True)
 
-    def put(buf, i, values):
-        buf[i] = jnp.zeros((8, 128), F32)
+    def put(buf, values):
+        buf[...] = jnp.zeros((8, 128), F32)
         for k, x in enumerate(values):
-            buf[i, pl.ds(k, 1), :] = jnp.broadcast_to(x, (1, 128))
-
-    def to_group(turn, k, q):
+            buf[pl.ds(k, 1), :] = jnp.broadcast_to(x, (1, 128))
+
+    def to_group(k, q):
         return pltpu.make_async_remote_copy(
-            src_ref=row.at[turn], dst_ref=tab.at[turn, q],
-            send_sem=ts.at[turn, k], recv_sem=tr.at[turn, q],
+            src_ref=row, dst_ref=tab.at[q], send_sem=ts.at[0, k], recv_sem=tr.at[0, q],
+            device_id={"dp": lax.rem(me + k, GROUP)}, device_id_type=MESH,
+        )
+
+    def one_to_group(k, q):
+        return pltpu.make_async_remote_copy(
+            src_ref=one_row, dst_ref=one_tab.at[q], send_sem=ts.at[1, k], recv_sem=tr.at[1, q],
             device_id={"dp": lax.rem(me + k, GROUP)}, device_id_type=MESH,
         )
 
@@ -424,21 +476,24 @@
             device_id={"mp": lax.rem(mx + k, N_MP)}, device_id_type=MESH,
         )
 
-    def exchange_send(turn, values):
-        put(row, turn, values)
+    def exchange_send(values):
+        put(row, values)
 
         @pl.loop(1, GROUP)
         def _(k):
-            to_group(turn, k, me).start()
-
-        tab[turn, me] = row[turn]
-
-    def exchange_middle(turn, middle):
+            to_group(k, me).start()
+
+        tab[me] = row[...]
+
+    def exchange_middle():
         @pl.loop(1, GROUP)
         def _(k):
-            to_group(turn, k, lax.rem(me + k, GROUP)).wait()
-
-        put(row2, turn, middle(tab[turn]))
+            to_group(k, lax.rem(me + k, GROUP)).wait()
+
+        put(row2.at[0], centre(tab[...]))
+        exchange_over_mp(0)
+
+    def exchange_over_mp(turn):
         for k in range(1, N_MP):
             to_mp(turn, k, mx).start()
         tab2[turn, mx] = row2[turn]
@@ -475,15 +530,14 @@
     u = gv - x * wv
     for j in range(BLOCKS):
         ag.drain(j)
-    exchange_send(0, (gg, gw, ww, total(u * u), total(u * wv), x))
+    exchange_send((gg, gw, ww, total(u * u), total(u * wv), x))
     xg.second(3)
     xg.third(2)
     drain(False)
-    exchange_middle(0, centre)
-    xg.third(3)
-    for i in range(4):
-        xg.drain(i)
-        xg.landed(i)
+    exchange_middle()
+    xg.drain(0)
+    xg.landed(0)
+    xg.landed(2)
     tb = exchange_end(0)
     norm = jnp.sum(column(tb, 0), axis=0)
     step = norm / jnp.sum(column(tb, 1), axis=0)
@@ -505,7 +559,8 @@
     drain(True)
     for j in (2, 3):
         ag.drain(j)
-        xg.drain(2 + j)
+        xg.drain(j)
+        lg.drain(j - 2)
 
 
 def shards(features, curvature, task_grad):
@@ -537,21 +592,30 @@
             pltpu.VMEM((BLOCKS, 16, ROWS, NB), F32),
             pltpu.VMEM((BLOCKS, 16, ROWS, NB), BF),
             pltpu.VMEM((BLOCKS, 3, RING, ROWS, NB), F32),
-            pltpu.VMEM((BLOCKS, 3, RING, ROWS, NB), BF),
             pltpu.VMEM((BLOCKS, RING, ROWS, NB), F32),
             pltpu.VMEM((BLOCKS, 3, ROWS, NB), F32),
-            pltpu.VMEM((6, ROWS, NB), F32),
-            pltpu.VMEM((6, 16, ROWS, NB), F32),
-            pltpu.VMEM((6, 16, ROWS, NB), F32),
+            pltpu.VMEM((BLOCKS, 16, ROWS, NB), BF),
+            pltpu.VMEM((4, ROWS, NB), F32),
+            pltpu.VMEM((4, 16, ROWS, NB), F32),
+            pltpu.VMEM((4, 16, ROWS, NB), F32),
+            pltpu.VMEM((2, ROWS, NB), BF),
+            pltpu.VMEM((2, 16, ROWS, NB), BF),
+            pltpu.VMEM((2, 16, ROWS, NB), BF),
             pltpu.VMEM(small, F32),
-            pltpu.VMEM((2, 8, 128), F32),
-            pltpu.VMEM((2, GROUP, 8, 128), F32),
+            pltpu.VMEM((8, 128), F32),
+            pltpu.VMEM((GROUP, 8, 128), F32),
+            pltpu.VMEM((1, 128), F32),
+            pltpu.VMEM((GROUP, 1, 128), F32),
             pltpu.VMEM((2, 8, 128), F32),
             pltpu.VMEM((2, N_MP, 8, 128), F32),
             pltpu.SemaphoreType.DMA((BLOCKS, 18)),
             pltpu.SemaphoreType.DMA((BLOCKS, 18)),
-            pltpu.SemaphoreType.DMA((6, 10)),
-            pltpu.SemaphoreType.DMA((6, 10)),
+            pltpu.SemaphoreType.DMA((4, 10)),
+            pltpu.SemaphoreType.DMA((4, 10)),
+            pltpu.SemaphoreType.DMA((2, 10)),
+            pltpu.SemaphoreType.DMA((2, 10)),
+            pltpu.SemaphoreType.DMA((BLOCKS, 16)),
+            pltpu.SemaphoreType.DMA((BLOCKS, 16)),
             pltpu.SemaphoreType.DMA((2, GROUP)),
             pltpu.SemaphoreType.DMA((2, GROUP)),
             pltpu.SemaphoreType.DMA((2, N_MP)),

time: 95.6 us -> 92.9 us (0.972)
  Pallas kernels: 93.6 us -> 90.7 us
    pallas_call x1, Pallas kernels: 93.6 us -> 90.7 us  [shards(): pl.pallas_call(kernel, out_shape=(out, out), in_specs=[any_spec] * 3, out...]
where the time goes in v4:
time: 92.9 us; the launch traced here: 92.6 us
  Pallas kernels  90.7 us (98%)
  local copies, waits for them, and re-layouts  1.31 us (1%)
    pallas_call x1, Pallas kernels, shards(): pl.pallas_call(kernel, out_shape=(out, out), in_specs=[any_spec] * 3, out...  90.7 us

profile of v4, /device:TPU:1, one launch (start us, length us, event | category | flops | bytes accessed | tf_op | source)
XLA Modules:
  0.0 92.6 jit_solution(18084850263731722515)
XLA Ops:
  0.6 90.7 %shard_map.50 = (f32[32,1024]{1,0:T(8,128)S(1)}, f32[32,1024]{1,0:T(8,128)S(1)}) custom-call(bf16[3072,1024]{1,0:T(8,128)(2,1)} %f_h.1, bf16[3072,1024]{1,0:T(8,128)(2,1)} %c_h.1, f32[32,1024]{1,0:T(8,128)} %g_h.1), custom_call_target="tpu_custom_call" | custom-call | tf_op jit(solution)/shard_map/pallas_call | solution.py:570
  91.3 0.7 copy.7
  92.0 0.7 copy.8

commit v5 on v4

--- a/solution.py
+++ b/solution.py
@@ -31,7 +31,7 @@
     f, ft, cv, g, d, w, sol, vb, g_own, g_par, v, wt,
     acc, accb, d0, d0b, s, sb, rin, t, r2in,
     din, xsrc, xo, xp, lsrc, lo, lp, pdv, row, tab, one_row, one_tab, row2, tab2,
-    ss, rs, xs, xr, ls, lr, ds, dr, ts, tr, ts2, tr2, ld,
+    gs, gr, qs, qr, es, er, ld,
 ):
     me = lax.axis_index("dp")
     mx = lax.axis_index("mp")
@@ -57,7 +57,7 @@
     qb_up, qb_dn, qb_op = lax.rem(pb + 1, RING), lax.rem(pb + 3, RING), lax.rem(pb + 2, RING)
 
     loads = [
-        pltpu.make_async_copy(g_h.at[:, pl.ds(j * NB, NB)], g.at[j], ld.at[j])
+        pltpu.make_async_copy(g_h.at[:, pl.ds(j * NB, NB)], g.at[j], ld.at[0])
         for j in range(BLOCKS)
     ]
     parts = 4
@@ -65,11 +65,11 @@
         pltpu.make_async_copy(
             f_h.at[pl.ds(k * (TOK // parts), TOK // parts)],
             f.at[pl.ds(k * (TOK // parts), TOK // parts)],
-            ld.at[BLOCKS + k],
+            ld.at[1 + k],
         )
         for k in range(parts)
     ]
-    c_load = pltpu.make_async_copy(c_h, cv, ld.at[BLOCKS + parts])
+    c_load = pltpu.make_async_copy(c_h, cv, ld.at[1 + parts])
     for x in (*loads, *f_loads, c_load):
         x.start()
 
@@ -83,69 +83,64 @@
             barrier, inc=1, device_id={"mp": lax.rem(mx + k, N_MP)}, device_id_type=MESH
         )
 
-    def copy(j, i, src, dst, dev):
+    def copy(src, dst, sends, recvs, dev):
         return pltpu.make_async_remote_copy(
-            src_ref=src, dst_ref=dst, send_sem=ss.at[j, i], recv_sem=rs.at[j, i],
+            src_ref=src, dst_ref=dst, send_sem=sends, recv_sem=recvs,
             device_id={"dp": dev}, device_id_type=MESH,
         )
 
     def send(j, i, src, dst, dev):
-        copy(j, i, src, dst, dev).start()
-
-    def got(j, i, dst):
-        copy(j, i, dst, dst, partner).wait_recv()
-
-    def sent(j, i, src):
-        copy(j, i, src, src, partner).wait_send()
+        copy(src, dst, qs.at[j, i], qr.at[j, i], dev).start()
+
+    def got(j, i, whole):
+        copy(whole, whole, qs.at[j, i], qr.at[j, i], partner).wait_recv()
+
+    def sent(j, i, whole):
+        copy(whole, whole, qs.at[j, i], qr.at[j, i], partner).wait_send()
 
     def strip(buf, j, q):
         return buf.at[j, pl.ds(q * RING, RING)]
 
     class Gather:
-        def __init__(self, src, own, par, sends, recvs):
-            self.src, self.own, self.par, self.sends, self.recvs = src, own, par, sends, recvs
+        def __init__(self, src, own, par, base):
+            self.src, self.own, self.par, self.base = src, own, par, base
 
         def copy(self, j, i, src, dst, dev):
-            return pltpu.make_async_remote_copy(
-                src_ref=src, dst_ref=dst, send_sem=self.sends.at[j, i], recv_sem=self.recvs.at[j, i],
-                device_id={"dp": dev}, device_id_type=MESH,
-            )
-
-        def got(self, j, i, dst):
-            self.copy(j, i, dst, dst, partner).wait_recv()
+            return copy(src, dst, gs.at[self.base + j, i], gr.at[self.base + j, i], dev)
+
+        def got(self, j, i, pieces):
+            part = self.own.at[j, pl.ds(0, pieces)]
+            self.copy(j, i, part, part, partner).wait_recv()
 
         def first(self, j):
             at = pb * RING + pa
-            for i, dev in enumerate((a_up, a_dn, a_op)):
-                self.copy(j, i, self.src.at[j], self.own.at[j, at], dev).start()
+            for dev in (a_up, a_dn, a_op):
+                self.copy(j, 0, self.src.at[j], self.own.at[j, at], dev).start()
             self.own[j, at] = self.src[j]
 
         def second(self, j):
-            for i, q in enumerate((qa_dn, qa_up, qa_op)):
-                self.got(j, i, self.own.at[j, pb * RING + q])
+            self.got(j, 0, 3)
             mine = strip(self.own, j, pb)
-            for i, dev in enumerate((b_up, b_dn, b_op)):
-                self.copy(j, 3 + i, mine, mine, dev).start()
-            self.copy(j, 6, mine, strip(self.par, j, pb), partner).start()
+            for dev in (b_up, b_dn, b_op):
+                self.copy(j, 1, mine, mine, dev).start()
+            self.copy(j, 2, mine, strip(self.par, j, pb), partner).start()
 
         def third(self, j):
-            for i, q in enumerate((qb_dn, qb_up, qb_op)):
-                part = strip(self.own, j, q)
-                self.got(j, 3 + i, part)
-                self.copy(j, 7 + i, part, strip(self.par, j, q), partner).start()
+            self.got(j, 1, 12)
+            for q in (qb_dn, qb_up, qb_op):
+                self.copy(j, 2, strip(self.own, j, q), strip(self.par, j, q), partner).start()
 
         def landed(self, j):
-            for i, q in enumerate((pa, qa_dn, qa_up, qa_op)):
-                self.got(j, 6 + i, strip(self.par, j, q))
+            self.got(j, 2, 16)
 
         def drain(self, j):
-            for i in range(10):
-                src = self.src.at[j] if i < 3 else strip(self.own, j, 0)
-                self.copy(j, i, src, src, partner).wait_send()
-
-    ag = Gather(vb, g_own, g_par, ss, rs)
-    xg = Gather(xsrc, xo, xp, xs, xr)
-    lg = Gather(lsrc, lo, lp, ls, lr)
+            for i, pieces in enumerate((3, 12, 16)):
+                part = self.own.at[j, pl.ds(0, pieces)]
+                self.copy(j, i, part, part, partner).wait_send()
+
+    ag = Gather(vb, g_own, g_par, 0)
+    xg = Gather(xsrc, xo, xp, BLOCKS)
+    lg = Gather(lsrc, lo, lp, BLOCKS + 4)
 
     def places():
         for zz in range(RING):
@@ -204,71 +199,57 @@
                 accb[j, zs] = out.astype(BF)
 
         src, dst = (accb, d0b) if low else (acc, d0)
-        send(j, 10 + h, src.at[j, zs, :, 1 - c], dst.at[j, zs], partner)
+        send(j, 0, src.at[j, zs, :, 1 - c], dst.at[j, zs], partner)
 
     def r1(j, low):
         src = d0b if low else d0
-        for h in range(2):
-            got(j, 10 + h, src.at[j, pl.ds(2 * h, 2)])
-            for zz in (2 * h, 2 * h + 1):
-                for yy in range(RING):
-                    zy, yz = zz * RING + yy, yy * RING + zz
-                    both = acc[j, zz, yy, c] + src[j, zz, yy].astype(F32)
-                    s[j, (1 - c) * yz + c * zy] = both
-                    if low:
-                        sb[j, (1 - c) * yz + c * zy] = both.astype(BF)
+        got(j, 0, src.at[j])
+        for zz, yy, _, at in places():
+            both = acc[j, zz, yy, c] + src[j, zz, yy].astype(F32)
+            s[j, at] = both
+            if low:
+                sb[j, at] = both.astype(BF)
         if low:
             for ka, kb in FAR_FIRST:
-                piece(j, ka, kb).start()
+                piece(j, ka, kb)
         else:
-            send(j, 12, strip(s, j, qa_up), rin.at[j, 0], a_up)
-            send(j, 13, strip(s, j, qa_dn), rin.at[j, 1], a_dn)
-            send(j, 14, strip(s, j, qa_op), rin.at[j, 2], a_op)
+            send(j, 1, strip(s, j, qa_up), rin.at[j, 0], a_up)
+            send(j, 1, strip(s, j, qa_dn), rin.at[j, 1], a_dn)
+            send(j, 1, strip(s, j, qa_op), rin.at[j, 2], a_op)
 
     def piece(j, ka, kb):
         qa, qb = lax.rem(pa + ka, RING), lax.rem(pb + kb, RING)
         dev = ((1 - c) * (qb * RING + qa) + c * (qa * RING + qb)) * 2 + c
-        return pltpu.make_async_remote_copy(
-            src_ref=sb.at[j, qa * RING + qb], dst_ref=din.at[j, ka * RING + kb],
-            send_sem=ds.at[j, ka * RING + kb], recv_sem=dr.at[j, ka * RING + kb],
-            device_id={"dp": dev}, device_id_type=MESH,
-        )
+        send(j, 3, sb.at[j, qa * RING + qb], din.at[j, ka * RING + kb], dev)
 
     def r4_low(j):
+        got(j, 3, din.at[j, pl.ds(1, 15)])
         total = s[j, pa * RING + pb]
-        for ka, kb in reversed(FAR_FIRST):
-            piece(j, ka, kb).wait_recv()
-            total += din[j, ka * RING + kb].astype(F32)
+        for k in range(1, 16):
+            total += din[j, k].astype(F32)
         w[j] = total / TOKENS + DAMP * d[j]
 
     def r3(j):
-        for i in range(3):
-            got(j, 12 + i, rin.at[j, i])
+        got(j, 1, rin.at[j])
         mine = s[j, pl.ds(pa * RING, RING)]
         t[j] = (mine + rin[j, 2]) + (rin[j, 0] + rin[j, 1])
-        send(j, 15, t.at[j, qb_up], r2in.at[j, 0], b_up)
-        send(j, 16, t.at[j, qb_dn], r2in.at[j, 1], b_dn)
-        send(j, 17, t.at[j, qb_op], r2in.at[j, 2], b_op)
+        send(j, 2, t.at[j, qb_up], r2in.at[j, 0], b_up)
+        send(j, 2, t.at[j, qb_dn], r2in.at[j, 1], b_dn)
+        send(j, 2, t.at[j, qb_op], r2in.at[j, 2], b_op)
 
     def r4(j):
-        for i in range(3):
-            got(j, 15 + i, r2in.at[j, i])
+        got(j, 2, r2in.at[j])
         total = (t[j, pb] + r2in[j, 2]) + (r2in[j, 0] + r2in[j, 1])
         w[j] = total / TOKENS + DAMP * d[j]
 
     def drain(low):
-        @pl.loop(0, BLOCKS)
-        def _(j):
-            for i in (10, 11):
-                sent(j, i, (d0b if low else d0).at[j, pl.ds(0, 2)])
+        for j in range(BLOCKS):
+            sent(j, 0, (d0b if low else d0).at[j])
             if low:
-                for ka, kb in FAR_FIRST:
-                    piece(j, ka, kb).wait_send()
+                sent(j, 3, din.at[j, pl.ds(1, 15)])
             else:
-                for i in (12, 13, 14):
-                    sent(j, i, rin.at[j, 0])
-                for i in (15, 16, 17):
-                    sent(j, i, t.at[j, 0])
+                sent(j, 1, rin.at[j])
+                sent(j, 2, r2in.at[j])
 
     def transpose(k0, k1):
         @pl.loop(k0, k1)
@@ -432,20 +413,12 @@
         value = total(pdv[...]) / TOKENS + DAMP * total(dv * dv)
         one_row[...] = jnp.broadcast_to(value, (1, 128))
 
-        @pl.loop(1, GROUP)
-        def _(k):
-            one_to_group(k, me).start()
-
-        one_tab[me] = one_row[...]
+        to_group(one_row, one_tab, 1)
         r1(last, True)
         r4_low(last - 2)
 
-        @pl.loop(1, GROUP)
-        def _(k):
-            one_to_group(k, lax.rem(me + k, GROUP)).wait()
-
-        put(row2.at[1], (jnp.sum(one_tab[...], axis=0),))
-        exchange_over_mp(1)
+        from_group(one_tab, 1)
+        to_mp(1, (jnp.sum(one_tab[...], axis=0),))
         r4_low(last - 1)
         r4_low(last)
 
@@ -457,50 +430,32 @@
         for k, x in enumerate(values):
             buf[pl.ds(k, 1), :] = jnp.broadcast_to(x, (1, 128))
 
-    def to_group(k, q):
+    def to_group(src, dst, i):
+        @pl.loop(1, GROUP)
+        def _(k):
+            copy(src, dst.at[me], es.at[i], er.at[i], lax.rem(me + k, GROUP)).start()
+
+        dst[me] = src[...]
+
+    def from_group(dst, i):
+        rest = dst.at[pl.ds(0, GROUP - 1)]
+        copy(rest, rest, es.at[i], er.at[i], partner).wait()
+
+    def over_mp(src, dst, i, k):
         return pltpu.make_async_remote_copy(
-            src_ref=row, dst_ref=tab.at[q], send_sem=ts.at[0, k], recv_sem=tr.at[0, q],
-            device_id={"dp": lax.rem(me + k, GROUP)}, device_id_type=MESH,
-        )
-
-    def one_to_group(k, q):
-        return pltpu.make_async_remote_copy(
-            src_ref=one_row, dst_ref=one_tab.at[q], send_sem=ts.at[1, k], recv_sem=tr.at[1, q],
-            device_id={"dp": lax.rem(me + k, GROUP)}, device_id_type=MESH,
-        )
-
-    def to_mp(turn, k, q):
-        return pltpu.make_async_remote_copy(
-            src_ref=row2.at[turn], dst_ref=tab2.at[turn, q],
-            send_sem=ts2.at[turn, k], recv_sem=tr2.at[turn, k],
+            src_ref=src, dst_ref=dst, send_sem=es.at[i], recv_sem=er.at[i],
             device_id={"mp": lax.rem(mx + k, N_MP)}, device_id_type=MESH,
         )
 
-    def exchange_send(values):
-        put(row, values)
-
-        @pl.loop(1, GROUP)
-        def _(k):
-            to_group(k, me).start()
-
-        tab[me] = row[...]
-
-    def exchange_middle():
-        @pl.loop(1, GROUP)
-        def _(k):
-            to_group(k, lax.rem(me + k, GROUP)).wait()
-
-        put(row2.at[0], centre(tab[...]))
-        exchange_over_mp(0)
-
-    def exchange_over_mp(turn):
+    def to_mp(turn, values):
+        put(row2.at[turn], values)
         for k in range(1, N_MP):
-            to_mp(turn, k, mx).start()
+            over_mp(row2.at[turn], tab2.at[turn, mx], 2 + turn, k).start()
         tab2[turn, mx] = row2[turn]
 
-    def exchange_end(turn):
-        for k in range(1, N_MP):
-            to_mp(turn, k, lax.rem(mx + N_MP - k, N_MP)).wait()
+    def from_mp(turn):
+        rest = tab2.at[turn, pl.ds(0, N_MP - 1)]
+        over_mp(rest, rest, 2 + turn, 1).wait()
         return tab2[turn]
 
     def column(tb, k):
@@ -520,8 +475,7 @@
         uu, uw = moved(tb, x)
         return gg, gw, ww, uu, uw, x
 
-    for x in loads:
-        x.wait()
+    pltpu.make_async_copy(g, g, ld.at[0]).wait()
     d[...] = g[...]
     operator_first()
     gv, wv = g[...], w[...]
@@ -530,15 +484,17 @@
     u = gv - x * wv
     for j in range(BLOCKS):
         ag.drain(j)
-    exchange_send((gg, gw, ww, total(u * u), total(u * wv), x))
+    put(row, (gg, gw, ww, total(u * u), total(u * wv), x))
+    to_group(row, tab, 0)
     xg.second(3)
     xg.third(2)
     drain(False)
-    exchange_middle()
+    from_group(tab, 0)
+    to_mp(0, centre(tab[...]))
     xg.drain(0)
     xg.landed(0)
     xg.landed(2)
-    tb = exchange_end(0)
+    tb = from_mp(0)
     norm = jnp.sum(column(tb, 0), axis=0)
     step = norm / jnp.sum(column(tb, 1), axis=0)
     norm_next, _ = moved(tb, step)
@@ -549,7 +505,7 @@
     g[...] = res
     d[...] = res + beta * gv
     operator_second(step, beta)
-    tb = exchange_end(1)
+    tb = from_mp(1)
     step = (norm_next / jnp.sum(column(tb, 0), axis=0))[:, :1]
     dv, wv = d[...], w[...]
     for j in range(BLOCKS):
@@ -608,19 +564,13 @@
             pltpu.VMEM((GROUP, 1, 128), F32),
             pltpu.VMEM((2, 8, 128), F32),
             pltpu.VMEM((2, N_MP, 8, 128), F32),
-            pltpu.SemaphoreType.DMA((BLOCKS, 18)),
-            pltpu.SemaphoreType.DMA((BLOCKS, 18)),
-            pltpu.SemaphoreType.DMA((4, 10)),
-            pltpu.SemaphoreType.DMA((4, 10)),
-            pltpu.SemaphoreType.DMA((2, 10)),
-            pltpu.SemaphoreType.DMA((2, 10)),
-            pltpu.SemaphoreType.DMA((BLOCKS, 16)),
-            pltpu.SemaphoreType.DMA((BLOCKS, 16)),
-            pltpu.SemaphoreType.DMA((2, GROUP)),
-            pltpu.SemaphoreType.DMA((2, GROUP)),
-            pltpu.SemaphoreType.DMA((2, N_MP)),
-            pltpu.SemaphoreType.DMA((2, N_MP)),
-            pltpu.SemaphoreType.DMA((2 * BLOCKS + 1,)),
+            pltpu.SemaphoreType.DMA((BLOCKS + 6, 3)),
+            pltpu.SemaphoreType.DMA((BLOCKS + 6, 3)),
+            pltpu.SemaphoreType.DMA((BLOCKS, 4)),
+            pltpu.SemaphoreType.DMA((BLOCKS, 4)),
+            pltpu.SemaphoreType.DMA((4,)),
+            pltpu.SemaphoreType.DMA((4,)),
+            pltpu.SemaphoreType.DMA((6,)),
         ],
         compiler_params=pltpu.CompilerParams(
             collective_id=0, has_side_effects=True, vmem_limit_bytes=51 * 2**20

time: 92.9 us -> 89.4 us (0.962)
  Pallas kernels: 90.7 us -> 87.4 us
    pallas_call x1, Pallas kernels: 90.7 us -> 87.4 us  [shards(): pl.pallas_call(kernel, out_shape=(out, out), in_specs=[any_spec] * 3, out...]
where the time goes in v5:
time: 89.4 us; the launch traced here: 89.3 us
  Pallas kernels  87.4 us (98%)
  local copies, waits for them, and re-layouts  1.31 us (1%)
    pallas_call x1, Pallas kernels, shards(): pl.pallas_call(kernel, out_shape=(out, out), in_specs=[any_spec] * 3, out...  87.4 us

profile of v5, /device:TPU:1, one launch (start us, length us, event | category | flops | bytes accessed | tf_op | source)
XLA Modules:
  0.0 89.3 jit_solution(8381472124436641019)
XLA Ops:
  0.6 87.4 %shard_map.50 = (f32[32,1024]{1,0:T(8,128)S(1)}, f32[32,1024]{1,0:T(8,128)S(1)}) custom-call(bf16[3072,1024]{1,0:T(8,128)(2,1)} %f_h.1, bf16[3072,1024]{1,0:T(8,128)(2,1)} %c_h.1, f32[32,1024]{1,0:T(8,128)} %g_h.1), custom_call_target="tpu_custom_call" | custom-call | tf_op jit(solution)/shard_map/pallas_call | solution.py:526
  88.0 0.7 copy.7
  88.7 0.7 copy.8

commit v6 on v5

--- a/solution.py
+++ b/solution.py
@@ -30,7 +30,7 @@
     f_h, c_h, g_h, sol_o, res_o,
     f, ft, cv, g, d, w, sol, vb, g_own, g_par, v, wt,
     acc, accb, d0, d0b, s, sb, rin, t, r2in,
-    din, xsrc, xo, xp, lsrc, lo, lp, pdv, row, tab, one_row, one_tab, row2, tab2,
+    din, xsrc, xo, xp, lsrc, lo, lp, pdv, row, tab, one_row, one_tab,
     gs, gr, qs, qr, es, er, ld,
 ):
     me = lax.axis_index("dp")
@@ -140,7 +140,7 @@
 
     ag = Gather(vb, g_own, g_par, 0)
     xg = Gather(xsrc, xo, xp, BLOCKS)
-    lg = Gather(lsrc, lo, lp, BLOCKS + 4)
+    lg = Gather(lsrc, lo, lp, 0)
 
     def places():
         for zz in range(RING):
@@ -186,20 +186,36 @@
             p = jnp.dot(f[...], v[j].reshape(DIN, NB), preferred_element_type=F32)
             wt[...] = (cv[:, cols].astype(F32) * p).astype(BF)
 
-    def p2(j, h, low):
-        r = pl.ds(h * (DIN // 2), DIN // 2)
-        zs = pl.ds(2 * h, 2)
+    def p2(j, z0, zn, low):
+        r = pl.ds(z0 * (DIN // RING), zn * (DIN // RING))
+        zs = pl.ds(z0, zn)
 
         @alone(j)
         def _(_):
             out = jnp.dot(ft[r, :], wt[...], preferred_element_type=F32)
-            out = out.reshape(2, RING, 2, ROWS, NB)
+            out = out.reshape(zn, RING, 2, ROWS, NB)
             acc[j, zs] = out
             if low:
                 accb[j, zs] = out.astype(BF)
 
         src, dst = (accb, d0b) if low else (acc, d0)
         send(j, 0, src.at[j, zs, :, 1 - c], dst.at[j, zs], partner)
+
+    def p2_start(j, low):
+        halves = j % 2 == 1 if low else j == BLOCKS - 1
+
+        @pl.when(~halves)
+        def _():
+            p2(j, 0, RING, low)
+
+        @pl.when(halves)
+        def _():
+            p2(j, 0, RING // 2, low)
+
+    def p2_end(j, low):
+        @pl.when(j % 2 == 1 if low else j == BLOCKS - 1)
+        def _():
+            p2(j, RING // 2, RING // 2, low)
 
     def r1(j, low):
         src = d0b if low else d0
@@ -220,10 +236,10 @@
     def piece(j, ka, kb):
         qa, qb = lax.rem(pa + ka, RING), lax.rem(pb + kb, RING)
         dev = ((1 - c) * (qb * RING + qa) + c * (qa * RING + qb)) * 2 + c
-        send(j, 3, sb.at[j, qa * RING + qb], din.at[j, ka * RING + kb], dev)
+        send(j, 1, sb.at[j, qa * RING + qb], din.at[j, ka * RING + kb], dev)
 
     def r4_low(j):
-        got(j, 3, din.at[j, pl.ds(1, 15)])
+        got(j, 1, din.at[j, pl.ds(1, 15)])
         total = s[j, pa * RING + pb]
         for k in range(1, 16):
             total += din[j, k].astype(F32)
@@ -246,7 +262,7 @@
         for j in range(BLOCKS):
             sent(j, 0, (d0b if low else d0).at[j])
             if low:
-                sent(j, 3, din.at[j, pl.ds(1, 15)])
+                sent(j, 1, din.at[j, pl.ds(1, 15)])
             else:
                 sent(j, 1, rin.at[j])
                 sent(j, 2, r2in.at[j])
@@ -300,11 +316,15 @@
                 xg.second(0)
                 xg.second(1)
 
-            p2(j, 0, False)
-
-            @pl.when(j >= 2)
-            def _():
-                r3(j - 2)
+            @pl.when(j == 3)
+            def _():
+                r3(0)
+
+            p2_start(j, False)
+
+            @pl.when(j == 3)
+            def _():
+                r3(1)
 
             @pl.when(j < BLOCKS - 1)
             def _():
@@ -314,16 +334,13 @@
             def _():
                 xg.third(j - 1)
 
-            @pl.when(j >= 3)
-            def _():
-                r4(j - 3)
-                xsrc[2] = w[0]
-                xg.first(2)
-
-            p2(j, 1, False)
+            p2_end(j, False)
 
         last = BLOCKS - 1
         r1(last, False)
+        r4(last - 3)
+        xsrc[2] = w[0]
+        xg.first(2)
         r3(last - 1)
         r4(last - 2)
         xsrc[3] = w[1]
@@ -354,7 +371,6 @@
 
             @pl.when(j == 1)
             def _():
-                ag.third(2)
                 pd(0)
 
             @pl.when(j == 2)
@@ -371,7 +387,7 @@
             def _():
                 r1(j - 1, True)
 
-            p2(j, 0, True)
+            p2_start(j, True)
 
             @pl.when(j == 0)
             def _():
@@ -384,6 +400,7 @@
 
             @pl.when(j == 1)
             def _():
+                ag.third(2)
                 ag.third(3)
 
             @pl.when(j == 2)
@@ -395,7 +412,7 @@
             def _():
                 r4_low(j - 3)
 
-            p2(j, 1, True)
+            p2_end(j, True)
 
             @pl.when(j == 0)
             def _():
@@ -413,67 +430,65 @@
         value = total(pdv[...]) / TOKENS + DAMP * total(dv * dv)
         one_row[...] = jnp.broadcast_to(value, (1, 128))
 
-        to_group(one_row, one_tab, 1)
+        to_far(one_row, one_tab, 1)
         r1(last, True)
+        to_near(one_row, one_tab, 1)
         r4_low(last - 2)
 
-        from_group(one_tab, 1)
-        to_mp(1, (jnp.sum(one_tab[...], axis=0),))
         r4_low(last - 1)
         r4_low(last)
+        from_all(one_tab, 1)
 
     def total(x):
         return jnp.sum(jnp.sum(jnp.sum(x, axis=0), axis=0, keepdims=True), axis=1, keepdims=True)
 
-    def put(buf, values):
-        buf[...] = jnp.zeros((8, 128), F32)
-        for k, x in enumerate(values):
-            buf[pl.ds(k, 1), :] = jnp.broadcast_to(x, (1, 128))
-
-    def to_group(src, dst, i):
+    def to_device(src, dst, i, dp, mp):
+        pltpu.make_async_remote_copy(
+            src_ref=src, dst_ref=dst.at[mx * GROUP + me], send_sem=es.at[i], recv_sem=er.at[i],
+            device_id={"dp": dp, "mp": mp}, device_id_type=MESH,
+        ).start()
+
+    def to_group(src, dst, i, k):
+        mp = lax.rem(mx + k, N_MP)
+
+        @pl.loop(0, GROUP, unroll=8)
+        def _(q):
+            to_device(src, dst, i, lax.rem(me + q + GROUP // 2 + 2, GROUP), mp)
+
+    def to_far(src, dst, i):
+        to_group(src, dst, i, 2)
+        to_group(src, dst, i, 1)
+
+    def to_near(src, dst, i):
+        to_group(src, dst, i, 3)
+
         @pl.loop(1, GROUP)
-        def _(k):
-            copy(src, dst.at[me], es.at[i], er.at[i], lax.rem(me + k, GROUP)).start()
-
-        dst[me] = src[...]
-
-    def from_group(dst, i):
-        rest = dst.at[pl.ds(0, GROUP - 1)]
+        def _(q):
+            to_device(src, dst, i, lax.rem(me + q, GROUP), mx)
+
+        dst[mx * GROUP + me] = src[...]
+
+    def from_all(dst, i):
+        rest = dst.at[pl.ds(0, GROUP * N_MP - 1)]
         copy(rest, rest, es.at[i], er.at[i], partner).wait()
 
-    def over_mp(src, dst, i, k):
-        return pltpu.make_async_remote_copy(
-            src_ref=src, dst_ref=dst, send_sem=es.at[i], recv_sem=er.at[i],
-            device_id={"mp": lax.rem(mx + k, N_MP)}, device_id_type=MESH,
-        )
-
-    def to_mp(turn, values):
-        put(row2.at[turn], values)
-        for k in range(1, N_MP):
-            over_mp(row2.at[turn], tab2.at[turn, mx], 2 + turn, k).start()
-        tab2[turn, mx] = row2[turn]
-
-    def from_mp(turn):
-        rest = tab2.at[turn, pl.ds(0, N_MP - 1)]
-        over_mp(rest, rest, 2 + turn, 1).wait()
-        return tab2[turn]
-
-    def column(tb, k):
-        return tb[:, k : k + 1, :]
-
-    def moved(tb, x):
-        ww, uu, uw, at = (column(tb, k) for k in (2, 3, 4, 5))
-        gap = at - x
-        return jnp.sum(uu + gap * (2.0 * uw + gap * ww), axis=0), jnp.sum(uw + gap * ww, axis=0)
+    lane = lax.broadcasted_iota(jnp.int32, (1, 128), 1)
+
+    def at_lane(x, k):
+        return jnp.sum(jnp.where(lane == k, x, 0.0), axis=1, keepdims=True)
+
+    def scalars(tb):
+        sums, x = tb[:, 0:1, :], tb[:, 1:2, :]
+        all_sums = jnp.sum(sums, axis=0)
+        norm = at_lane(all_sums, 3)
+        step = norm / at_lane(all_sums, 4)
+        gap = x - step[None]
+        at = lane[None]
+        factor = jnp.where(at == 0, 1.0, jnp.where(at == 1, gap, jnp.where(at == 2, gap * gap, 0.0)))
+        return norm, step, jnp.sum(jnp.sum(sums * factor, axis=0), axis=1, keepdims=True)
 
     def ratio(p, q):
         return jnp.where(q > 0, p / jnp.where(q > 0, q, 1.0), 0.0)
-
-    def centre(tb):
-        gg, gw, ww = (jnp.sum(column(tb, k), axis=0) for k in range(3))
-        x = ratio(gw, ww)
-        uu, uw = moved(tb, x)
-        return gg, gw, ww, uu, uw, x
 
     pltpu.make_async_copy(g, g, ld.at[0]).wait()
     d[...] = g[...]
@@ -484,29 +499,28 @@
     u = gv - x * wv
     for j in range(BLOCKS):
         ag.drain(j)
-    put(row, (gg, gw, ww, total(u * u), total(u * wv), x))
-    to_group(row, tab, 0)
+    packed = jnp.zeros((1, 128), F32)
+    for k, value in enumerate((total(u * u), 2.0 * total(u * wv), ww, gg, gw)):
+        packed = jnp.where(lane == k, value, packed)
+    row[0:1, :] = packed
+    row[1:2, :] = jnp.broadcast_to(x, (1, 128))
+    to_far(row, tab, 0)
+    to_near(row, tab, 0)
     xg.second(3)
     xg.third(2)
     drain(False)
-    from_group(tab, 0)
-    to_mp(0, centre(tab[...]))
     xg.drain(0)
     xg.landed(0)
     xg.landed(2)
-    tb = from_mp(0)
-    norm = jnp.sum(column(tb, 0), axis=0)
-    step = norm / jnp.sum(column(tb, 1), axis=0)
-    norm_next, _ = moved(tb, step)
-    beta = (norm_next / norm)[:, :1]
-    step = step[:, :1]
+    from_all(tab, 0)
+    norm, step, norm_next = scalars(tab[...])
+    beta = norm_next / norm
     sol[...] = step * gv
     res = gv - step * wv
     g[...] = res
     d[...] = res + beta * gv
     operator_second(step, beta)
-    tb = from_mp(1)
-    step = (norm_next / jnp.sum(column(tb, 0), axis=0))[:, :1]
+    step = norm_next / jnp.sum(one_tab[...], axis=0)[:, :1]
     dv, wv = d[...], w[...]
     for j in range(BLOCKS):
         cols = pl.ds(j * NB, NB)
@@ -558,18 +572,16 @@
             pltpu.VMEM((2, 16, ROWS, NB), BF),
             pltpu.VMEM((2, 16, ROWS, NB), BF),
             pltpu.VMEM(small, F32),
-            pltpu.VMEM((8, 128), F32),
-            pltpu.VMEM((GROUP, 8, 128), F32),
+            pltpu.VMEM((2, 128), F32),
+            pltpu.VMEM((GROUP * N_MP, 2, 128), F32),
             pltpu.VMEM((1, 128), F32),
-            pltpu.VMEM((GROUP, 1, 128), F32),
-            pltpu.VMEM((2, 8, 128), F32),
-            pltpu.VMEM((2, N_MP, 8, 128), F32),
-            pltpu.SemaphoreType.DMA((BLOCKS + 6, 3)),
-            pltpu.SemaphoreType.DMA((BLOCKS + 6, 3)),
-            pltpu.SemaphoreType.DMA((BLOCKS, 4)),
-            pltpu.SemaphoreType.DMA((BLOCKS, 4)),
-            pltpu.SemaphoreType.DMA((4,)),
-            pltpu.SemaphoreType.DMA((4,)),
+            pltpu.VMEM((GROUP * N_MP, 1, 128), F32),
+            pltpu.SemaphoreType.DMA((BLOCKS + 4, 3)),
+            pltpu.SemaphoreType.DMA((BLOCKS + 4, 3)),
+            pltpu.SemaphoreType.DMA((BLOCKS, 3)),
+            pltpu.SemaphoreType.DMA((BLOCKS, 3)),
+            pltpu.SemaphoreType.DMA((2,)),
+            pltpu.SemaphoreType.DMA((2,)),
             pltpu.SemaphoreType.DMA((6,)),
         ],
         compiler_params=pltpu.CompilerParams(

time: 89.4 us -> 85.2 us (0.953)
  Pallas kernels: 87.4 us -> 83.2 us
    pallas_call x1, Pallas kernels: 87.4 us -> 83.2 us  [shards(): pl.pallas_call(kernel, out_shape=(out, out), in_specs=[any_spec] * 3, out...]
where the time goes in v6:
time: 85.2 us; the launch traced here: 85.1 us
  Pallas kernels  83.2 us (98%)
  local copies, waits for them, and re-layouts  1.31 us (2%)
    pallas_call x1, Pallas kernels, shards(): pl.pallas_call(kernel, out_shape=(out, out), in_specs=[any_spec] * 3, out...  83.2 us

profile of v6, /device:TPU:1, one launch (start us, length us, event | category | flops | bytes accessed | tf_op | source)
XLA Modules:
  0.0 85.1 jit_solution(8709881519108774636)
XLA Ops:
  0.6 83.2 %shard_map.50 = (f32[32,1024]{1,0:T(8,128)S(1)}, f32[32,1024]{1,0:T(8,128)S(1)}) custom-call(bf16[3072,1024]{1,0:T(8,128)(2,1)} %f_h.1, bf16[3072,1024]{1,0:T(8,128)(2,1)} %c_h.1, f32[32,1024]{1,0:T(8,128)} %g_h.1), custom_call_target="tpu_custom_call" | custom-call | tf_op jit(solution)/shard_map/pallas_call | solution.py:540
  83.8 0.7 copy.7
  84.5 0.7 copy.8

commit v7 on v6

--- a/solution.py
+++ b/solution.py
@@ -186,7 +186,7 @@
             p = jnp.dot(f[...], v[j].reshape(DIN, NB), preferred_element_type=F32)
             wt[...] = (cv[:, cols].astype(F32) * p).astype(BF)
 
-    def p2(j, z0, zn, low):
+    def p2(j, z0, zn, low, i=0):
         r = pl.ds(z0 * (DIN // RING), zn * (DIN // RING))
         zs = pl.ds(z0, zn)
 
@@ -199,7 +199,7 @@
                 accb[j, zs] = out.astype(BF)
 
         src, dst = (accb, d0b) if low else (acc, d0)
-        send(j, 0, src.at[j, zs, :, 1 - c], dst.at[j, zs], partner)
+        send(j, i, src.at[j, zs, :, 1 - c], dst.at[j, zs], partner)
 
     def p2_start(j, low):
         halves = j % 2 == 1 if low else j == BLOCKS - 1
@@ -215,7 +215,7 @@
     def p2_end(j, low):
         @pl.when(j % 2 == 1 if low else j == BLOCKS - 1)
         def _():
-            p2(j, RING // 2, RING // 2, low)
+            p2(j, RING // 2, RING // 2, low, 2 * (j // (BLOCKS - 1)) if low else 0)
 
     def r1(j, low):
         src = d0b if low else d0
@@ -233,6 +233,22 @@
             send(j, 1, strip(s, j, qa_dn), rin.at[j, 1], a_dn)
             send(j, 1, strip(s, j, qa_op), rin.at[j, 2], a_op)
 
+    def r1_half(j, h):
+        got(j, 2 * h, d0b.at[j, pl.ds(2 * h, 2)])
+        for zz, yy, _, at in places():
+            if zz // 2 == h:
+                both = acc[j, zz, yy, c] + d0b[j, zz, yy].astype(F32)
+                s[j, at] = both
+                sb[j, at] = both.astype(BF)
+        for zz, yy, _, at in places():
+            if zz // 2 == h:
+
+                @pl.when((zz != z) | (yy != y))
+                def _(zz=zz, yy=yy, at=at):
+                    ka = lax.rem((1 - c) * yy + c * zz + RING - pa, RING)
+                    kb = lax.rem((1 - c) * zz + c * yy + RING - pb, RING)
+                    send(j, 1, sb.at[j, at], din.at[j, ka * RING + kb], (zz * RING + yy) * 2 + c)
+
     def piece(j, ka, kb):
         qa, qb = lax.rem(pa + ka, RING), lax.rem(pb + kb, RING)
         dev = ((1 - c) * (qb * RING + qa) + c * (qa * RING + qb)) * 2 + c
@@ -260,7 +276,11 @@
 
     def drain(low):
         for j in range(BLOCKS):
-            sent(j, 0, (d0b if low else d0).at[j])
+            if low and j == BLOCKS - 1:
+                for h in range(2):
+                    sent(j, 2 * h, d0b.at[j, pl.ds(2 * h, 2)])
+            else:
+                sent(j, 0, (d0b if low else d0).at[j])
             if low:
                 sent(j, 1, din.at[j, pl.ds(1, 15)])
             else:
@@ -424,6 +444,7 @@
                 fill(2)
 
         last = BLOCKS - 1
+        r1_half(last, 0)
         lg.landed(1)
         pd_rest(3)
         dv = d[...]
@@ -431,8 +452,8 @@
         one_row[...] = jnp.broadcast_to(value, (1, 128))
 
         to_far(one_row, one_tab, 1)
-        r1(last, True)
         to_near(one_row, one_tab, 1)
+        r1_half(last, 1)
         r4_low(last - 2)
 
         r4_low(last - 1)

time: 85.2 us -> 83.9 us (0.985)
  Pallas kernels: 83.2 us -> 81.8 us
    pallas_call x1, Pallas kernels: 83.2 us -> 81.8 us  [shards(): pl.pallas_call(kernel, out_shape=(out, out), in_specs=[any_spec] * 3, out...]
where the time goes in v7:
time: 83.9 us; the launch traced here: 83.8 us
  Pallas kernels  81.8 us (97%)
  local copies, waits for them, and re-layouts  1.31 us (2%)
    pallas_call x1, Pallas kernels, shards(): pl.pallas_call(kernel, out_shape=(out, out), in_specs=[any_spec] * 3, out...  81.8 us

profile of v7, /device:TPU:1, one launch (start us, length us, event | category | flops | bytes accessed | tf_op | source)
XLA Modules:
  0.0 83.8 jit_solution(9552300567965077836)
XLA Ops:
  0.6 81.8 %shard_map.50 = (f32[32,1024]{1,0:T(8,128)S(1)}, f32[32,1024]{1,0:T(8,128)S(1)}) custom-call(bf16[3072,1024]{1,0:T(8,128)(2,1)} %f_h.1, bf16[3072,1024]{1,0:T(8,128)(2,1)} %c_h.1, f32[32,1024]{1,0:T(8,128)} %g_h.1), custom_call_target="tpu_custom_call" | custom-call | tf_op jit(solution)/shard_map/pallas_call | solution.py:561
  82.5 0.7 copy.7
  83.1 0.7 copy.8

commit v8 on v7

--- a/solution.py
+++ b/solution.py
@@ -215,7 +215,7 @@
     def p2_end(j, low):
         @pl.when(j % 2 == 1 if low else j == BLOCKS - 1)
         def _():
-            p2(j, RING // 2, RING // 2, low, 2 * (j // (BLOCKS - 1)) if low else 0)
+            p2(j, RING // 2, RING // 2, low, 3 * (j // (BLOCKS - 1)))
 
     def r1(j, low):
         src = d0b if low else d0
@@ -233,8 +233,30 @@
             send(j, 1, strip(s, j, qa_dn), rin.at[j, 1], a_dn)
             send(j, 1, strip(s, j, qa_op), rin.at[j, 2], a_op)
 
+    def r1_part(j, h):
+        got(j, 3 * h, d0.at[j, pl.ds(2 * h, 2)])
+        for zz, yy, _, at in places():
+            if zz // 2 == h:
+                s[j, at] = acc[j, zz, yy, c] + d0[j, zz, yy]
+
+        @pl.when(c == 0)
+        def _():
+            for i, (q, dev) in enumerate(((qa_up, a_up), (qa_dn, a_dn), (qa_op, a_op))):
+                part = s.at[j, pl.ds(q * RING + 2 * h, 2)]
+                send(j, 1, part, rin.at[j, i, pl.ds(2 * h, 2)], dev)
+
+        @pl.when(c == 1)
+        def _():
+            for q in (2 * h, 2 * h + 1):
+
+                @pl.when(pa != q)
+                def _(q=q):
+                    ka = lax.rem(q + RING - pa, RING)
+                    slot = lax.rem(2 * (ka + 2), 3)
+                    send(j, 1, s.at[j, pl.ds(q * RING, RING)], rin.at[j, slot], (q * RING + y) * 2 + c)
+
     def r1_half(j, h):
-        got(j, 2 * h, d0b.at[j, pl.ds(2 * h, 2)])
+        got(j, 3 * h, d0b.at[j, pl.ds(2 * h, 2)])
         for zz, yy, _, at in places():
             if zz // 2 == h:
                 both = acc[j, zz, yy, c] + d0b[j, zz, yy].astype(F32)
@@ -276,11 +298,12 @@
 
     def drain(low):
         for j in range(BLOCKS):
-            if low and j == BLOCKS - 1:
+            src = d0b if low else d0
+            if j == BLOCKS - 1:
                 for h in range(2):
-                    sent(j, 2 * h, d0b.at[j, pl.ds(2 * h, 2)])
+                    sent(j, 3 * h, src.at[j, pl.ds(2 * h, 2)])
             else:
-                sent(j, 0, (d0b if low else d0).at[j])
+                sent(j, 0, src.at[j])
             if low:
                 sent(j, 1, din.at[j, pl.ds(1, 15)])
             else:
@@ -357,7 +380,8 @@
             p2_end(j, False)
 
         last = BLOCKS - 1
-        r1(last, False)
+        r1_part(last, 0)
+        r1_part(last, 1)
         r4(last - 3)
         xsrc[2] = w[0]
         xg.first(2)
@@ -599,8 +623,8 @@
             pltpu.VMEM((GROUP * N_MP, 1, 128), F32),
             pltpu.SemaphoreType.DMA((BLOCKS + 4, 3)),
             pltpu.SemaphoreType.DMA((BLOCKS + 4, 3)),
-            pltpu.SemaphoreType.DMA((BLOCKS, 3)),
-            pltpu.SemaphoreType.DMA((BLOCKS, 3)),
+            pltpu.SemaphoreType.DMA((BLOCKS, 4)),
+            pltpu.SemaphoreType.DMA((BLOCKS, 4)),
             pltpu.SemaphoreType.DMA((2,)),
             pltpu.SemaphoreType.DMA((2,)),
             pltpu.SemaphoreType.DMA((6,)),

time: 83.9 us -> 83.6 us (level)
  no operation moved by 1% of the time
where the time goes in v8:
time: 83.6 us; the launch traced here: 83.5 us
  Pallas kernels  81.5 us (97%)
  local copies, waits for them, and re-layouts  1.31 us (2%)
    pallas_call x1, Pallas kernels, shards(): pl.pallas_call(kernel, out_shape=(out, out), in_specs=[any_spec] * 3, out...  81.5 us

profile of v8, /device:TPU:1, one launch (start us, length us, event | category | flops | bytes accessed | tf_op | source)
XLA Modules:
  0.0 83.5 jit_solution(12741070810621002617)
XLA Ops:
  0.6 81.5 %shard_map.50 = (f32[32,1024]{1,0:T(8,128)S(1)}, f32[32,1024]{1,0:T(8,128)S(1)}) custom-call(bf16[3072,1024]{1,0:T(8,128)(2,1)} %f_h.1, bf16[3072,1024]{1,0:T(8,128)(2,1)} %c_h.1, f32[32,1024]{1,0:T(8,128)} %g_h.1), custom_call_target="tpu_custom_call" | custom-call | tf_op jit(solution)/shard_map/pallas_call | solution.py:585
  82.2 0.7 copy.7
  82.8 0.7 copy.8
